TPU v7x, 32 devices: a whole 2x2x4 slice. The times are simulated.
32 devices in a mesh: dp: 4 (over y, x), fsdp: 8 (over z, core).
Axes of the slice: x: 2, y: 2, z: 4, core: 2. Of those that a mesh axis runs over, the one named last changes fastest.
Arguments:
- tokens_in: bfloat16 [32, 1024, 768], P(('dp', 'fsdp')), may hold values from -6 to 6
- ln1_gain: bfloat16 [768], P('fsdp'), may hold values from 0.5 to 1.5
- ln1_bias: bfloat16 [768], P('fsdp'), may hold values from -3 to 3
- ln2_gain: bfloat16 [768], P('fsdp'), may hold values from 0.5 to 1.5
- ln2_bias: bfloat16 [768], P('fsdp'), may hold values from -3 to 3
- qkv_weight: bfloat16 [768, 2304], P('fsdp'), may hold values from -0.21875 to 0.21875
- qkv_bias: bfloat16 [2304], P('fsdp'), may hold values from -2 to 2
- out_weight: bfloat16 [768, 768], P('fsdp'), may hold values from -0.625 to 0.625
- out_bias: bfloat16 [768], P('fsdp'), may hold values from -2 to 2
- up_weight: bfloat16 [768, 3072], P('fsdp'), may hold values from -0.21875 to 0.21875
- up_bias: bfloat16 [3072], P('fsdp'), may hold values from -2 to 2
- down_weight: bfloat16 [3072, 768], P('fsdp'), may hold values from -0.15625 to 0.15625
- down_bias: bfloat16 [768], P('fsdp'), may hold values from -2 to 2
- cotangent: bfloat16 [32, 1024, 768], P(('dp', 'fsdp')), may hold values from -6 to 6
- lengths: int32 [32], P(('dp', 'fsdp')), may hold values from 128 to 1024, as said below
- assignment: int32 [32], P(('dp', 'fsdp')), may hold values from 0 to 31, each once
- clip_bound: int32 [1], replicated, may hold values from 6 to 10
Outputs:
- mixed: bfloat16 [32, 1024, 768], P(('dp', 'fsdp'))
- tokens_grad: bfloat16 [32, 1024, 768], P(('dp', 'fsdp'))
- clip_scale: float32 [32], replicated
- ln1_gain_grad: float32 [768], P('fsdp')
- ln1_bias_grad: float32 [768], P('fsdp')
- ln2_gain_grad: float32 [768], P('fsdp')
- ln2_bias_grad: float32 [768], P('fsdp')
- qkv_weight_grad: float32 [768, 2304], P('fsdp')
- qkv_bias_grad: float32 [2304], P('fsdp')
- out_weight_grad: float32 [768, 768], P('fsdp')
- out_bias_grad: float32 [768], P('fsdp')
- up_weight_grad: float32 [768, 3072], P('fsdp')
- up_bias_grad: float32 [3072], P('fsdp')
- down_weight_grad: float32 [3072, 768], P('fsdp')
- down_bias_grad: float32 [768], P('fsdp')
Inputs may be any that keep to these rules, and one draw needn't show every extreme that they name: `lengths`: every slot's length lies between 128 and 1024; both ends occur in every draw. `assignment`: each example number occurs once.
All inputs are finite; a program needn't handle non-finite values.
Results may differ from a plain program's by a relative error of at most 0.0095.
Values may be sent and summed in bfloat16 or wider, within the bound.
No kernel may reach another device: no remote copies, remote signals or barrier semaphores. Data moves between devices by JAX's collectives and lax.ppermute only.
A program may use at most 256 MiB of HBM per device.

v0:
```python
import math

import jax
import jax.numpy as jnp
from jax import lax
from jax.sharding import PartitionSpec as P

D = 768
HEADS = 12
HEAD_DIM = 64
ROT_DIM = 16


def product_tn(left, right):
    return lax.dot_general(
        left, right, (((0,), (0,)), ((), ())), preferred_element_type=jnp.float32
    )


def product_nt(left, right):
    return lax.dot_general(
        left, right, (((1,), (1,)), ((), ())), preferred_element_type=jnp.float32
    )


def norm_forward(values, gain, shift):
    row_mean = jnp.mean(values, -1, keepdims=True)
    centred = values - row_mean
    inverse = lax.rsqrt(jnp.mean(centred * centred, -1, keepdims=True) + 1e-05)
    normed = centred * inverse
    return (normed, inverse, normed * gain + shift)


def norm_backward(upstream, normed, inverse, gain):
    scaled = upstream * gain
    spread = (
        scaled
        - jnp.mean(scaled, -1, keepdims=True)
        - normed * jnp.mean(scaled * normed, -1, keepdims=True)
    )
    return (jnp.sum(upstream * normed, 0), jnp.sum(upstream, 0), inverse * spread)


def rotary_tables(count):
    positions = jnp.arange(count).astype(jnp.float32)
    inverse = 10000.0 ** (-jnp.arange(0, ROT_DIM, 2).astype(jnp.float32) / ROT_DIM)
    angles = positions[:, None] * inverse[None, :]
    angles = jnp.concatenate([angles, angles], -1)
    return (jnp.cos(angles)[:, None, :], jnp.sin(angles)[:, None, :])


def rotate_part(block, cosine, sine):
    half_dim = ROT_DIM // 2
    front = block[..., :ROT_DIM]
    turned = jnp.concatenate([-front[..., half_dim:], front[..., :half_dim]], -1)
    return jnp.concatenate([front * cosine + turned * sine, block[..., ROT_DIM:]], -1)


def rotate_back(block, cosine, sine):
    half_dim = ROT_DIM // 2
    front = block[..., :ROT_DIM]
    moved = front * sine
    unturned = jnp.concatenate([moved[..., half_dim:], -moved[..., :half_dim]], -1)
    return jnp.concatenate([front * cosine + unturned, block[..., ROT_DIM:]], -1)


def body(
    tokens_in,
    ln1_gain,
    ln1_bias,
    ln2_gain,
    ln2_bias,
    qkv_weight,
    qkv_bias,
    out_weight,
    out_bias,
    up_weight,
    up_bias,
    down_weight,
    down_bias,
    cotangent,
    lengths,
    assignment,
    clip_bound,
):
    gathered = (
        lax.all_gather(ln1_gain, "fsdp", axis=0, tiled=True),
        lax.all_gather(ln1_bias, "fsdp", axis=0, tiled=True),
        lax.all_gather(ln2_gain, "fsdp", axis=0, tiled=True),
        lax.all_gather(ln2_bias, "fsdp", axis=0, tiled=True),
        lax.all_gather(qkv_weight, "fsdp", axis=0, tiled=True),
        lax.all_gather(qkv_bias, "fsdp", axis=0, tiled=True),
        lax.all_gather(out_weight, "fsdp", axis=0, tiled=True),
        lax.all_gather(out_bias, "fsdp", axis=0, tiled=True),
        lax.all_gather(up_weight, "fsdp", axis=0, tiled=True),
        lax.all_gather(up_bias, "fsdp", axis=0, tiled=True),
        lax.all_gather(down_weight, "fsdp", axis=0, tiled=True),
        lax.all_gather(down_bias, "fsdp", axis=0, tiled=True),
    )
    f32 = jnp.float32
    bf16 = jnp.bfloat16
    tokens = tokens_in[0].astype(f32)
    count = tokens.shape[0]
    length = lengths[0]
    positions = jnp.arange(count, dtype=jnp.int32)
    valid_rows = (positions < length).astype(f32)[:, None]
    normed_one, inverse_one, first_full = norm_forward(
        tokens, gathered[0].astype(f32), gathered[1].astype(f32)
    )
    normed_two, inverse_two, second_full = norm_forward(
        tokens, gathered[2].astype(f32), gathered[3].astype(f32)
    )
    first = first_full.astype(bf16)
    second = second_full.astype(bf16)
    packed = (
        jnp.dot(first, gathered[4], preferred_element_type=f32) + gathered[5].astype(f32)
    ).reshape(count, HEADS, 3 * HEAD_DIM)
    cosine, sine = rotary_tables(count)
    queries = rotate_part(packed[..., :HEAD_DIM], cosine, sine).astype(bf16)
    keys_rot = rotate_part(packed[..., HEAD_DIM : 2 * HEAD_DIM], cosine, sine).astype(bf16)
    values_all = packed[..., 2 * HEAD_DIM :].astype(bf16)
    factor_score = HEAD_DIM ** (-0.5)
    block_rows = min(512, count)
    block_count = count // block_rows

    def block_scores(start):
        row_ids = positions[start : start + block_rows]
        scores = (
            jnp.einsum(
                "qhd,khd->hqk",
                queries[start : start + block_rows],
                keys_rot,
                preferred_element_type=f32,
            )
            * factor_score
        )
        allowed = (positions[None, :] <= row_ids[:, None]) & (positions[None, :] < length)
        return jnp.where(allowed[None], scores, -1e30)

    head_parts = []
    log_totals = []
    for block_index in range(block_count):
        scores = block_scores(block_index * block_rows)
        highest = jnp.max(scores, -1, keepdims=True)
        raised = jnp.exp(scores - highest)
        denominator = jnp.sum(raised, -1, keepdims=True)
        probs = raised / denominator
        log_totals.append(highest + jnp.log(denominator))
        head_parts.append(
            jnp.einsum("hqk,khd->qhd", probs.astype(bf16), values_all, preferred_element_type=f32)
        )
    heads_out = jnp.concatenate(head_parts, 0).reshape(count, D).astype(bf16)
    attention = jnp.dot(heads_out, gathered[6], preferred_element_type=f32) + gathered[7].astype(
        f32
    )
    inner = jnp.dot(second, gathered[8], preferred_element_type=f32) + gathered[9].astype(f32)
    activated = jax.nn.gelu(inner, approximate=False).astype(bf16)
    feed = jnp.dot(activated, gathered[10], preferred_element_type=f32) + gathered[11].astype(f32)
    mixed = (valid_rows * (tokens + attention + feed)).astype(bf16)[None]
    back_set = (
        lax.all_gather(ln1_gain, "fsdp", axis=0, tiled=True),
        lax.all_gather(ln1_bias, "fsdp", axis=0, tiled=True),
        lax.all_gather(ln2_gain, "fsdp", axis=0, tiled=True),
        lax.all_gather(ln2_bias, "fsdp", axis=0, tiled=True),
        lax.all_gather(qkv_weight, "fsdp", axis=0, tiled=True),
        lax.all_gather(qkv_bias, "fsdp", axis=0, tiled=True),
        lax.all_gather(out_weight, "fsdp", axis=0, tiled=True),
        lax.all_gather(out_bias, "fsdp", axis=0, tiled=True),
        lax.all_gather(up_weight, "fsdp", axis=0, tiled=True),
        lax.all_gather(up_bias, "fsdp", axis=0, tiled=True),
        lax.all_gather(down_weight, "fsdp", axis=0, tiled=True),
        lax.all_gather(down_bias, "fsdp", axis=0, tiled=True),
    )
    upstream = jnp.where(valid_rows > 0, cotangent[0], jnp.zeros_like(cotangent[0]))
    upstream_full = upstream.astype(f32)
    bias_grad = jnp.sum(upstream_full, 0)
    out_weight_grad = product_tn(heads_out, upstream)
    down_weight_grad = product_tn(activated, upstream)
    head_grad = product_nt(upstream, back_set[6]).astype(bf16).reshape(count, HEADS, HEAD_DIM)
    act_grad = product_nt(upstream, back_set[10])
    normal_cdf = 0.5 * (1.0 + lax.erf(inner * math.sqrt(0.5)))
    normal_pdf = jnp.exp(-0.5 * inner * inner) / math.sqrt(2.0 * math.pi)
    inner_grad = (act_grad * (normal_cdf + inner * normal_pdf)).astype(bf16)
    up_bias_grad = jnp.sum(inner_grad.astype(f32), 0)
    up_weight_grad = product_tn(second, inner_grad)
    second_grad = product_nt(inner_grad, back_set[8])
    query_parts = []
    key_grad = jnp.zeros((count, HEADS, HEAD_DIM), f32)
    value_grad = jnp.zeros((count, HEADS, HEAD_DIM), f32)
    for block_index in range(block_count):
        start = block_index * block_rows
        probs = jnp.exp(block_scores(start) - log_totals[block_index])
        head_block = head_grad[start : start + block_rows]
        prob_grad = jnp.einsum("qhd,khd->hqk", head_block, values_all, preferred_element_type=f32)
        row_dot = jnp.sum(probs * prob_grad, -1, keepdims=True)
        score_grad = (probs * (prob_grad - row_dot)).astype(bf16)
        query_parts.append(
            jnp.einsum("hqk,khd->qhd", score_grad, keys_rot, preferred_element_type=f32)
            * factor_score
        )
        key_grad = (
            key_grad
            + jnp.einsum(
                "hqk,qhd->khd",
                score_grad,
                queries[start : start + block_rows],
                preferred_element_type=f32,
            )
            * factor_score
        )
        value_grad = value_grad + jnp.einsum(
            "hqk,qhd->khd", probs.astype(bf16), head_block, preferred_element_type=f32
        )
    query_grad = rotate_back(jnp.concatenate(query_parts, 0), cosine, sine)
    key_grad = rotate_back(key_grad, cosine, sine)
    packed_grad = (
        jnp.concatenate([query_grad, key_grad, value_grad], -1).reshape(count, 3 * D).astype(bf16)
    )
    qkv_bias_grad = jnp.sum(packed_grad.astype(f32), 0)
    qkv_weight_grad = product_tn(first, packed_grad)
    first_grad = product_nt(packed_grad, back_set[4])
    gain_one_grad, shift_one_grad, input_one = norm_backward(
        first_grad, normed_one, inverse_one, back_set[0].astype(f32)
    )
    gain_two_grad, shift_two_grad, input_two = norm_backward(
        second_grad, normed_two, inverse_two, back_set[2].astype(f32)
    )
    token_grad = upstream_full + input_one + input_two
    grads = (
        gain_one_grad,
        shift_one_grad,
        gain_two_grad,
        shift_two_grad,
        qkv_weight_grad,
        qkv_bias_grad,
        out_weight_grad,
        bias_grad,
        up_weight_grad,
        up_bias_grad,
        down_weight_grad,
        bias_grad,
    )
    squares = sum((jnp.sum(entry * entry) for entry in grads))
    dp_count = lax.axis_size("dp")
    fsdp_count = lax.axis_size("fsdp")
    total_count = dp_count * fsdp_count
    slot_ids = jnp.arange(total_count, dtype=jnp.int32)
    mine = slot_ids == assignment[0]
    square_vector = lax.psum(jnp.where(mine, squares, jnp.float32(0.0)), ("dp", "fsdp"))
    norms = jnp.sqrt(square_vector)
    median = jnp.sort(norms)[total_count // 2]
    bound = median * clip_bound[0].astype(f32) / 8.0
    clip_scale = jnp.minimum(1.0, bound / (norms + 1e-06))
    own_scale = jnp.sum(jnp.where(mine, clip_scale, jnp.float32(0.0)))
    token_out = (own_scale * token_grad).astype(bf16)[None]
    weight_scale = own_scale / total_count
    scaled = tuple((entry * weight_scale for entry in grads))
    owned = (
        lax.psum_scatter(scaled[0], "fsdp", scatter_dimension=0, tiled=True),
        lax.psum_scatter(scaled[1], "fsdp", scatter_dimension=0, tiled=True),
        lax.psum_scatter(scaled[2], "fsdp", scatter_dimension=0, tiled=True),
        lax.psum_scatter(scaled[3], "fsdp", scatter_dimension=0, tiled=True),
        lax.psum_scatter(scaled[4], "fsdp", scatter_dimension=0, tiled=True),
        lax.psum_scatter(scaled[5], "fsdp", scatter_dimension=0, tiled=True),
        lax.psum_scatter(scaled[6], "fsdp", scatter_dimension=0, tiled=True),
        lax.psum_scatter(scaled[7], "fsdp", scatter_dimension=0, tiled=True),
        lax.psum_scatter(scaled[8], "fsdp", scatter_dimension=0, tiled=True),
        lax.psum_scatter(scaled[9], "fsdp", scatter_dimension=0, tiled=True),
        lax.psum_scatter(scaled[10], "fsdp", scatter_dimension=0, tiled=True),
        lax.psum_scatter(scaled[11], "fsdp", scatter_dimension=0, tiled=True),
    )
    reduced = lax.psum(
        (
            owned[0],
            owned[1],
            owned[2],
            owned[3],
            owned[4],
            owned[5],
            owned[6],
            owned[7],
            owned[8],
            owned[9],
            owned[10],
            owned[11],
        ),
        "dp",
    )
    return (mixed, token_out, clip_scale) + tuple(reduced)


def solution(mesh):
    return jax.shard_map(
        body,
        mesh=mesh,
        in_specs=(
            P(("dp", "fsdp"), None, None),
            P("fsdp"),
            P("fsdp"),
            P("fsdp"),
            P("fsdp"),
            P("fsdp", None),
            P("fsdp"),
            P("fsdp", None),
            P("fsdp"),
            P("fsdp", None),
            P("fsdp"),
            P("fsdp", None),
            P("fsdp"),
            P(("dp", "fsdp"), None, None),
            P(("dp", "fsdp")),
            P(("dp", "fsdp")),
            P(),
        ),
        out_specs=(
            P(("dp", "fsdp"), None, None),
            P(("dp", "fsdp"), None, None),
            P(),
            P("fsdp"),
            P("fsdp"),
            P("fsdp"),
            P("fsdp"),
            P("fsdp", None),
            P("fsdp"),
            P("fsdp", None),
            P("fsdp"),
            P("fsdp", None),
            P("fsdp"),
            P("fsdp", None),
            P("fsdp"),
        ),
        check_vma=False,
    )
```

profile of v0, /device:TPU:0, one launch (start us, length us, event | category | flops | bytes accessed | tf_op | source)
XLA Modules:
  0.0 902.1 jit_solution(16282463421792579940)
XLA Ops:
  18.6 31.3 %all-reduce.17 = (bf16[768]{0:T(1024)(128)(2,1)S(1)}, bf16[768]{0:T(1024)(128)(2,1)S(1)}, bf16[768]{0:T(1024)(128)(2,1)}, bf16[768]{0:T(1024)(128)(2,1)}, bf16[2...) all-reduce(bf16[768]{0:T(1024)(128)(2,1)S(1)} %dynamic-update-slice, ...), channel_id=1, replica_groups=mesh['dp'=4,'fsdp'=8] {'fsdp'}, use_global_device_ids=true, to_apply=%add.5 | all-reduce | flops 6912 | bytes 27648
  56.5 13.3 %all-gather = bf16[8,1,384]{2,1,0:T(2,128)(2,1)S(1)} all-gather(bf16[1,1,384]{2,1,0:T(2,128)(2,1)S(1)} %reshape.315), channel_id=1, replica_groups=mesh['dp'=4,'fsdp'=8] {'fsdp'}, dimensions={0}, use_global_device_ids=true | all-gather | bytes 6912 | tf_op jit(solution)/shard_map/all_gather | solution.py:96
  74.2 3.4 convolution_convert_fusion
  79.0 8.8 convolution_add_fusion
  87.8 9.7 %copy.41 = f32[1024,2304]{0,1:T(8,128)} copy(f32[1024,2304]{1,0:T(8,128)} %convolution_add_fusion) | data formatting | bytes 18874368 | tf_op jit(solution)/shard_map/add | solution.py:116
  98.9 4.5 convert.23
  104.3 2.9 fusion.101
  107.3 10.7 %fusion.28 = (f32[12,512]{1,0:T(8,128)S(1)}, f32[12,512,1024]{2,1,0:T(8,128)}) fusion(pred[512,1024]{1,0:T(8,128)(4,1)S(1)} %copy-done.6, bf16[1024,12,48]{0,2,1:T(8,128)(2,1)S(1)} %get-tuple-element.65, bf16[1024,12,16]{0,2,1:T(8,128)(2,1)S(1)} %get-tuple-element.59, bf16[1024,12,16]{0,2,1:T(8,128)(2,1)S(1)} %get-tuple-element.60, ...), kind=kOutput, calls=%fused_computation.52 | convolution fusion | flops 828893184 | bytes 28860416 | tf_op jit(solution)/shard_map/qhd,khd->hqk/dot_general | solution.py:129
  118.1 11.9 %fusion = f32[12,512]{1,0:T(8,128)S(1)} fusion(f32[12,512]{1,0:T(8,128)S(1)} %get-tuple-element.84, f32[12,512,1024]{2,1,0:T(8,128)} %get-tuple-element.85, pred[512,1024]{1,0:T(8,128)(4,1)S(1)} %copy-done.6), kind=kLoop, calls=%fused_computation.12 | loop fusion | flops 25159680 | bytes 25739264 | tf_op jit(solution)/shard_map/reduce_sum | solution.py:146
  130.0 11.1 %fusion.29 = (f32[12,512]{1,0:T(8,128)S(1)}, f32[12,512,1024]{2,1,0:T(8,128)}) fusion(pred[512,1024]{1,0:T(8,128)(4,1)S(1)} %get-tuple-element.77, bf16[1024,12,48]{0,2,1:T(8,128)(2,1)S(1)} %get-tuple-element.65, bf16[1024,12,16]{0,2,1:T(8,128)(2,1)S(1)} %get-tuple-element.59, bf16[1024,12,48]{0,2,1:T(8,128)(2,1)S(1)} %get-tuple-element.66, ...), kind=kOutput, calls=%fused_computation.53 | convolution fusion | flops 828893184 | bytes 28860416 | tf_op jit(solution)/shard_map/qhd,khd->hqk/dot_general | solution.py:129
  141.1 12.0 %fusion.1 = f32[12,512]{1,0:T(8,128)S(1)} fusion(f32[12,512]{1,0:T(8,128)S(1)} %get-tuple-element.82, f32[12,512,1024]{2,1,0:T(8,128)} %get-tuple-element.83, pred[512,1024]{1,0:T(8,128)(4,1)S(1)} %get-tuple-element.77), kind=kLoop, calls=%fused_computation.13 | loop fusion | flops 25159680 | bytes 25739264 | tf_op jit(solution)/shard_map/reduce_sum | solution.py:146
  153.7 21.1 %multiply_reduce_fusion.1 = (f32[12,512]{1,0:T(8,128)}, f32[12,512,1024]{2,1,0:T(8,128)}) fusion(f32[12,512]{1,0:T(8,128)S(1)} %log_add_fusion.1, f32[12,512,1024]{2,1,0:T(8,128)} %get-tuple-element.85, pred[512,1024]{1,0:T(8,128)(4,1)S(1)} %copy-done.6, bf16[512,12,64]{0,2,1:T(8,128)(2,1)S(1)} %bitcast.169, bf16[1024,12,192]{0,2,1:T(8,128)(2,1)} %copy-done), kind=kOutput, calls=%fused_computation.4 | convolution fusion | flops 836757504 | bytes 53264384 | tf_op jit(solution)/shard_map/qhd,khd->hqk/dot_general | solution.py:194
  174.7 18.2 %multiply_reduce_fusion = (f32[12,512]{1,0:T(8,128)S(1)}, f32[12,512,1024]{2,1,0:T(8,128)}) fusion(f32[12,512]{1,0:T(8,128)S(1)} %log_add_fusion, f32[12,512,1024]{2,1,0:T(8,128)} %get-tuple-element.83, pred[512,1024]{1,0:T(8,128)(4,1)S(1)} %get-tuple-element.77, bf16[512,12,64]{0,2,1:T(8,128)(2,1)} %bitcast.171, bf16[1024,12,192]{0,2,1:T(8,128)(2,1)} %copy-done), kind=kOutput, calls=%fused_computation.1 | convolution fusion | flops 836757504 | bytes 53264384 | tf_op jit(solution)/shard_map/qhd,khd->hqk/dot_general | solution.py:194
  192.9 42.0 %multiply_convert_fusion = (bf16[12,512,1024]{2,1,0:T(8,128)(2,1)}, bf16[12,512,1024]{2,1,0:T(8,128)(2,1)}) fusion(f32[12,512,1024]{2,1,0:T(8,128)} %get-tuple-element.87, f32[12,512]{1,0:T(8,128)S(1)} %get-tuple-element.86, f32[12,512]{1,0:T(8,128)S(1)} %log_add_fusion, f32[12,512,1024]{2,1,0:T(8,128)} %get-tuple-element.83, ...), kind=kLoop, calls=%fused_computation | loop fusion | flops 75497472 | bytes 126976000 | tf_op jit(solution)/shard_map/convert_element_type | solution.py:196
  235.0 7.0 fusion.125
  242.0 9.6 %multiply_bitcast_fusion.2 = f32[512,12,64]{0,2,1:T(8,128)} fusion(bf16[12,512,1024]{2,1,0:T(8,128)(2,1)} %get-tuple-element.102, bf16[1024,12,48]{0,2,1:T(8,128)(2,1)S(1)} %copy-done.2, bf16[1024,12,16]{0,2,1:T(8,128)(2,1)S(1)} %copy-done.10), kind=kOutput, calls=%fused_computation.130 | convolution fusion | flops 808845312 | bytes 15728640 | tf_op jit(solution)/shard_map/hqk,khd->qhd/dot_general | solution.py:198
  251.7 13.4 %fusion.13 = f32[12,64,1024]{2,1,0:T(8,128)} fusion(bf16[512,12,64]{0,2,1:T(8,128)(2,1)} %bitcast.172, f32[12,512]{1,0:T(8,128)S(1)} %log_add_fusion, f32[12,512,1024]{2,1,0:T(8,128)} %get-tuple-element.83, pred[512,1024]{1,0:T(8,128)(4,1)S(1)} %get-tuple-element.77), kind=kOutput, calls=%fused_computation.27 | convolution fusion | flops 830472192 | bytes 29646848 | tf_op jit(solution)/shard_map/hqk,qhd->khd/dot_general | solution.py:211
  265.2 13.7 %fusion.92 = bf16[12,64,512]{2,1,0:T(8,128)(2,1)} fusion(f32[12,512]{1,0:T(8,128)} %copy-done.30, f32[12,512]{1,0:T(8,128)} %copy-done.29, f32[12,512,1024]{2,1,0:T(8,128)} %get-tuple-element.85, pred[512,1024]{1,0:T(8,128)(4,1)} %get-tuple-element.76, bf16[1024,12,192]{0,2,1:T(8,128)(2,1)} %copy-done), kind=kOutput, calls=%fused_computation.139 | convolution fusion | flops 837156864 | bytes 28114944 | tf_op jit(solution)/shard_map/hqk,khd->qhd/dot_general | solution.py:150
  280.4 10.1 %fusion.91 = bf16[12,64,512]{2,1,0:T(8,128)(2,1)} fusion(f32[12,512]{1,0:T(8,128)S(1)} %copy-done.32, f32[12,512]{1,0:T(8,128)S(1)} %get-tuple-element.82, f32[12,512,1024]{2,1,0:T(8,128)S(1)} %bitcast.161, pred[512,1024]{1,0:T(8,128)(4,1)S(1)} %get-tuple-element.77, bf16[1024,12,192]{0,2,1:T(8,128)(2,1)} %copy-done), kind=kOutput, calls=%fused_computation.138 | convolution fusion | flops 837156864 | bytes 28098560 | tf_op jit(solution)/shard_map/hqk,khd->qhd/dot_general | solution.py:150
  290.4 9.0 multiply_bitcast_fusion.1
  299.4 7.1 multiply_bitcast_fusion
  308.8 13.0 %bitcast_dynamic-update-slice_fusion = bf16[1024,12,192]{0,2,1:T(8,128)(2,1)S(1)} fusion(bf16[1024,12,192]{0,2,1:T(8,128)(2,1)S(1)} %slice_dynamic-update-slice_fusion, f32[12,64,1024]{2,1,0:T(8,128)} %fusion.13, bf16[512,12,64]{0,2,1:T(8,128)(2,1)S(1)} %bitcast.170, f32[12,512]{1,0:T(8,128)S(1)} %log_add_fusion.1, f32[12,512,1024]{2,1,0:T(8,128)} %get-tuple-element.85, ...), kind=kOutput, calls=%fused_computation.99 | convolution fusion | flops 831258624 | bytes 32800768 | tf_op jit(solution)/shard_map/hqk,qhd->khd/dot_general | solution.py:211
  322.0 7.7 multiply_reduce_fusion.4
  329.6 3.6 multiply_reduce_fusion.7
  335.2 37.4 %fusion.6 = (bf16[1024,3072]{1,0:T(8,128)(2,1)}, f32[1024,3072]{1,0:T(8,128)}) fusion(f32[3072]{0:T(1024)S(1)} %bitcast.178, bf16[768,3072]{1,0:T(8,128)(2,1)} %all-gather.10.cloned.1.call-done, bf16[1,1024,768]{2,1,0:T(8,128)(2,1)S(1)} %copy-done.4, f32[768]{0:T(1024)S(1)} %copy-done.45, f32[768]{0:T(1024)S(1)} %copy-done.41, f32[1024]{0:T(1024)S(1)} %copy-done.40, ...), kind=kOutput, calls=%fused_computation.20 | convolution fusion | flops 5044174848 | bytes 25192448 | tf_op jit(solution)/shard_map/dot_general | solution.py:156
  372.6 12.3 %convert_reduce_fusion = (f32[3072]{0:T(1024)S(1)}, bf16[1024,3072]{1,0:T(8,128)(2,1)S(1)}) fusion(f32[1024,3072]{1,0:T(8,128)} %get-tuple-element.81, f32[3072]{0:T(1024)S(1)} %bitcast.179, bf16[3072,768]{1,0:T(8,128)(2,1)} %all-gather.12.cloned.1.call-done, bf16[1,1024,768]{2,1,0:T(8,128)(2,1)S(1)} %copy-done.12, pred[1024]{0:T(1024)(128)(4,1)S(1)} %copy-done.47), kind=kOutput, calls=%fused_computation.29 | convolution fusion | flops 4873516032 | bytes 25191424 | tf_op jit(solution)/shard_map/dot_general | solution.py:21
  385.0 9.8 %multiply_reduce_fusion.3 = (f32[]{:T(128)}, f32[768,3072]{1,0:T(8,128)}) fusion(bf16[1024,3072]{1,0:T(8,128)(2,1)S(1)} %get-tuple-element.98, bf16[1,1024,768]{2,1,0:T(8,128)(2,1)S(1)} %copy-done.4, f32[768]{0:T(1024)S(1)} %copy-done.45, f32[768]{0:T(1024)S(1)} %copy-done.41, f32[1024]{0:T(1024)S(1)} %copy-done.40, f32[1024]{0:T(1024)S(1)} %copy-done.34), kind=kOutput, calls=%fused_computation.50 | convolution fusion | flops 4841275392 | bytes 17315844 | tf_op jit(solution)/shard_map/dot_general | solution.py:15
  394.8 5.1 fusion.139
  399.9 7.5 fusion.46
  410.5 11.4 %multiply_reduce_fusion.2 = (f32[]{:T(128)}, f32[3072,768]{1,0:T(8,128)}) fusion(bf16[1024,3072]{1,0:T(8,128)(2,1)} %get-tuple-element.80, bf16[1,1024,768]{2,1,0:T(8,128)(2,1)S(1)} %copy-done.12, pred[1024]{0:T(1024)(128)(4,1)S(1)} %copy-done.47), kind=kOutput, calls=%fused_computation.49 | convolution fusion | flops 4837343232 | bytes 17302532 | tf_op jit(solution)/shard_map/dot_general | solution.py:15
  429.5 38.9 %psum.87 = f32[32]{0:T(128)S(1)} all-reduce(f32[32]{0:T(128)S(1)} %compare_select_fusion.1), channel_id=1, replica_groups=mesh['dp'=4,'fsdp'=8] {'dp','fsdp'}, use_global_device_ids=true, to_apply=%region_26.27 | all-reduce | flops 32 | bytes 256 | tf_op jit(solution)/shard_map/psum | solution.py:249
  473.1 3.3 broadcast_multiply_fusion.3
  476.4 6.3 broadcast_multiply_fusion.2
  482.8 8.0 broadcast_multiply_fusion
  490.9 9.0 %broadcast_multiply_fusion.1 = f32[768,3072]{1,0:T(8,128)} fusion(f32[768,3072]{1,0:T(8,128)} %get-tuple-element.96, f32[]{:T(128)S(6)} %div.78), kind=kLoop, calls=%fused_computation.60 | loop fusion | flops 2359296 | bytes 18874372 | tf_op jit(solution)/shard_map/mul | solution.py:257
  502.0 2.7 pad_maximum_fusion.2
  504.8 8.6 reduce-scatter.7.cloned.1.call-done
  513.4 78.2 %reduce-scatter.5.cloned.1.call-done = f32[96,2304]{1,0:T(8,128)} async-done(((f32[768,2304]{1,0:T(8,128)}), f32[96,2304]{1,0:T(8,128)}) %reduce-scatter.5.cloned.1.call-update) | async-done | bytes 884752 | tf_op jit(solution)/shard_map/reduce_scatter | solution.py:263
  591.6 100.2 %reduce-scatter.11.cloned.1.call-done = f32[384,768]{1,0:T(8,128)} async-done(((f32[3072,768]{1,0:T(8,128)}), f32[384,768]{1,0:T(8,128)}) %reduce-scatter.11.cloned.1.call-update) | async-done | bytes 1179664 | tf_op jit(solution)/shard_map/reduce_scatter | solution.py:269
  691.8 100.2 %reduce-scatter.9.cloned.1.call-done = f32[96,3072]{1,0:T(8,128)} async-done(((f32[768,3072]{1,0:T(8,128)}), f32[96,3072]{1,0:T(8,128)}) %reduce-scatter.9.cloned.1.call-update) | async-done | bytes 1179664 | tf_op jit(solution)/shard_map/reduce_scatter | solution.py:267
  792.2 26.4 %all-reduce.14 = (f32[768]{0:T(1024)S(1)}, f32[768]{0:T(1024)S(1)}, f32[768]{0:T(1024)S(1)}, f32[768]{0:T(1024)S(1)}, f32[2304]{0:T(1024)S(1)}, /*index=5*/f32[768]{0:T(1024)S(1)}, f32[3072]{0:T(1024)S(1)}) all-reduce(f32[768]{0:T(1024)S(1)} %broadcast_multiply_fusion.12, ...), channel_id=2, replica_groups=mesh['dp'=4,'fsdp'=8] {'fsdp'}, use_global_device_ids=true, to_apply=%region_33.34.clone | all-reduce | flops 9216 | bytes 73728
  819.1 10.6 %all-reduce.15 = (f32[96]{0:T(128)}, f32[96]{0:T(128)}, f32[96]{0:T(128)}, f32[96]{0:T(128)}, f32[288]{0:T(512)}, /*index=5*/f32[96]{0:T(128)S(1)}, f32[384]{0:T(512)}) all-reduce(f32[96]{0:T(128)S(1)} %dynamic-slice.8, f32[96]{0:T(128)S(1)} %dynamic-slice.10, f32[96]{0:T(128)S(1)} %dynamic-slice.12, ...), channel_id=1, replica_groups=mesh['dp'=4,'fsdp'=8] {'dp'}, use_global_device_ids=true, to_apply=%region_34.35 | all-reduce | flops 1152 | bytes 9216 | tf_op jit(solution)/shard_map/psum | solution.py:272
  829.8 8.7 fusion.138
  838.5 3.1 fusion.90
  841.5 3.9 fusion.89
  845.4 42.2 %all-reduce.20.cloned.1.call-done = (f32[96,2304]{1,0:T(8,128)}, f32[96,768]{1,0:T(8,128)}, f32[96,3072]{1,0:T(8,128)}, f32[384,768]{1,0:T(8,128)}) async-done(((f32[96,2304]{1,0:T(8,128)}, f32[96,768]{1,0:T(8,128)}, f32[96,3072]{1,0:T(8,128)}, f32[384,768]{1,0:T(8,128)}), (f32[96,2304]{1,0:T(8,128)}, f32[96,768]{1,0:T(8,128)}, f32[96,3072]{1,0:T(8,128)}, ...) | async-done | bytes 3538960 | tf_op jit(solution)/shard_map/psum | solution.py:272
  888.2 2.1 copy.62
  892.0 2.4 copy.64
  (239 shorter events, 39.5 us)
Async XLA Ops:
  7.2 49.3 %copy-start.50 = (bf16[384]{0:T(512)(128)(2,1)S(1)}, bf16[384]{0:T(512)(128)(2,1)}, u32[]{:S(2)}) copy-start(bf16[384]{0:T(512)(128)(2,1)} %param.27) | copy-start | bytes 2308
  7.2 63.2 %copy-start.11 = (bf16[1,1024,768]{2,1,0:T(8,128)(2,1)S(1)}, bf16[1,1024,768]{2,1,0:T(8,128)(2,1)}, u32[]{:S(2)}) copy-start(bf16[1,1024,768]{2,1,0:T(8,128)(2,1)} %param.30) | copy-start | bytes 4718596
  7.2 67.0 %all-gather.8.cloned.1.call-start = ((), (), s32[]{:S(2)}) async-start(), calls=%async_computation.5 | async-start | bytes 1327104 | tf_op jit(solution)/shard_map/all_gather | solution.py:93
  7.9 71.0 %all-gather.6.cloned.1.call-start = ((), (), s32[]{:S(2)}) async-start(), calls=%async_computation.4 | async-start | bytes 3981312 | tf_op jit(solution)/shard_map/all_gather | solution.py:91
  8.7 326.5 %all-gather.10.cloned.1.call-start = ((), (), s32[]{:S(2)}) async-start(), calls=%async_computation.6 | async-start | bytes 5308416 | tf_op jit(solution)/shard_map/all_gather | solution.py:95
  9.4 363.2 %all-gather.12.cloned.1.call-start = ((), (), s32[]{:S(2)}) async-start(), calls=%async_computation.7 | async-start | bytes 5308416 | tf_op jit(solution)/shard_map/all_gather | solution.py:97
  10.0 503.4 %reduce-scatter.7.cloned.1.call-start = ((), (), s32[]{:S(2)}) async-start(), calls=%async_computation.9 | async-start | bytes 2654208 | tf_op jit(solution)/shard_map/reduce_scatter | solution.py:265
  49.9 29.0 %copy-start.37 = (f32[768]{0:T(1024)}, f32[768]{0:T(1024)S(1)}, u32[]{:S(2)}) copy-start(f32[768]{0:T(1024)S(1)} %convert_element_type.145) | copy-start | bytes 9220
  49.9 29.0 %copy-start.43 = (f32[768]{0:T(1024)}, f32[768]{0:T(1024)S(1)}, u32[]{:S(2)}) copy-start(f32[768]{0:T(1024)S(1)} %convert_element_type.146) | copy-start | bytes 9220
  51.6 27.3 %copy-start.33 = (f32[1024]{0:T(1024)}, f32[1024]{0:T(1024)S(1)}, u32[]{:S(2)}) copy-start(f32[1024]{0:T(1024)S(1)} %broadcast_multiply_fusion.17) | copy-start | bytes 12292
  53.7 25.2 %copy-start.39 = (f32[1024]{0:T(1024)}, f32[1024]{0:T(1024)S(1)}, u32[]{:S(2)}) copy-start(f32[1024]{0:T(1024)S(1)} %add_rsqrt_fusion) | copy-start | bytes 12292
  54.6 49.2 %copy-start.20 = (f32[1024,16]{0,1:T(8,128)}, f32[1024,16]{0,1:T(8,128)S(1)}, u32[]{:S(2)}) copy-start(f32[1024,16]{0,1:T(8,128)S(1)} %get-tuple-element.74) | copy-start | bytes 196612
  55.3 22.4 %copy-start.46 = (pred[1024]{0:T(1024)(128)(4,1)}, pred[1024]{0:T(1024)(128)(4,1)S(1)}, u32[]{:S(2)}) copy-start(pred[1024]{0:T(1024)(128)(4,1)S(1)} %broadcast_compare_fusion) | copy-start | bytes 3076
  103.4 14.6 %copy-start = (bf16[1024,12,192]{0,2,1:T(8,128)(2,1)}, bf16[1024,12,192]{0,2,1:T(8,128)(2,1)S(1)}, u32[]{:S(2)}) copy-start(bf16[1024,12,192]{0,2,1:T(8,128)(2,1)S(1)} %convert.23) | copy-start | bytes 14155780
  103.7 26.2 %copy-start.1 = (bf16[1024,12,48]{0,2,1:T(8,128)(2,1)}, bf16[1024,12,48]{0,2,1:T(8,128)(2,1)S(1)}, u32[]{:S(2)}) copy-start(bf16[1024,12,48]{0,2,1:T(8,128)(2,1)S(1)} %get-tuple-element.65) | copy-start | bytes 3538948
  107.3 22.7 %copy-start.9 = (bf16[1024,12,16]{0,2,1:T(8,128)(2,1)}, bf16[1024,12,16]{0,2,1:T(8,128)(2,1)S(1)}, u32[]{:S(2)}) copy-start(bf16[1024,12,16]{0,2,1:T(8,128)(2,1)S(1)} %get-tuple-element.59) | copy-start | bytes 1179652
  118.1 11.9 %copy-start.29 = (f32[12,512]{1,0:T(8,128)}, f32[12,512]{1,0:T(8,128)S(1)}, u32[]{:S(2)}) copy-start(f32[12,512]{1,0:T(8,128)S(1)} %get-tuple-element.84) | copy-start | bytes 73732
  129.9 11.1 %copy-start.30 = (f32[12,512]{1,0:T(8,128)}, f32[12,512]{1,0:T(8,128)S(1)}, u32[]{:S(2)}) copy-start(f32[12,512]{1,0:T(8,128)S(1)} %fusion) | copy-start | bytes 73732
  141.1 12.6 %copy-start.16 = (bf16[512,768]{0,1:T(8,128)(2,1)S(1)}, bf16[512,768]{0,1:T(8,128)(2,1)}, u32[]{:S(2)}) copy-start(bf16[512,768]{0,1:T(8,128)(2,1)} %get-tuple-element.67) | copy-start | bytes 2359300
  174.7 18.2 %copy-start.28 = (f32[12,512]{1,0:T(8,128)S(1)}, f32[12,512]{1,0:T(8,128)}, u32[]{:S(2)}) copy-start(f32[12,512]{1,0:T(8,128)} %get-tuple-element.88) | copy-start | bytes 73732
  251.7 27.1 %slice-start = ((s8[25165824]{0:T(1024)(128)(4,1)}), s8[4194304]{0:T(1024)(128)(4,1)S(1)}, s32[]{:S(2)}) async-start(s8[25165824]{0:T(1024)(128)(4,1)} %bitcast.160), calls=%async_computation.13 | async-start | bytes 8388608
  265.1 13.7 %slice-start.1 = ((s8[25165824]{0:T(1024)(128)(4,1)}), s8[4194304]{0:T(1024)(128)(4,1)S(1)}, s32[]{:S(2)}) async-start(s8[25165824]{0:T(1024)(128)(4,1)} %bitcast.160), calls=%async_computation.14 | async-start | bytes 8388608
  265.1 13.7 %slice-start.2 = ((s8[25165824]{0:T(1024)(128)(4,1)}), s8[4194304]{0:T(1024)(128)(4,1)S(1)}, s32[]{:S(2)}) async-start(s8[25165824]{0:T(1024)(128)(4,1)} %bitcast.160), calls=%async_computation.15 | async-start | bytes 8388608
  265.1 13.7 %slice-start.3 = ((s8[25165824]{0:T(1024)(128)(4,1)}), s8[4194304]{0:T(1024)(128)(4,1)S(1)}, s32[]{:S(2)}) async-start(s8[25165824]{0:T(1024)(128)(4,1)} %bitcast.160), calls=%async_computation.16 | async-start | bytes 8388608
  265.1 13.9 %slice-start.4 = ((s8[25165824]{0:T(1024)(128)(4,1)}), s8[4194304]{0:T(1024)(128)(4,1)S(1)}, s32[]{:S(2)}) async-start(s8[25165824]{0:T(1024)(128)(4,1)} %bitcast.160), calls=%async_computation.17 | async-start | bytes 8388608
  265.2 15.2 %slice-start.5 = ((s8[25165824]{0:T(1024)(128)(4,1)}), s8[4194304]{0:T(1024)(128)(4,1)S(1)}, s32[]{:S(2)}) async-start(s8[25165824]{0:T(1024)(128)(4,1)} %bitcast.160), calls=%async_computation.18 | async-start | bytes 8388608
  265.2 15.2 %copy-start.32 = (f32[12,512]{1,0:T(8,128)S(1)}, f32[12,512]{1,0:T(8,128)}, u32[]{:S(2)}) copy-start(f32[12,512]{1,0:T(8,128)} %copy-done.31) | copy-start | bytes 73732
  308.8 13.1 %copy-start.4 = (bf16[1,1024,768]{2,1,0:T(8,128)(2,1)S(1)}, bf16[1,1024,768]{2,1,0:T(8,128)(2,1)}, u32[]{:S(2)}) copy-start(bf16[1,1024,768]{2,1,0:T(8,128)(2,1)} %param.17) | copy-start | bytes 4718596
  308.8 13.1 %copy-start.34 = (f32[1024]{0:T(1024)S(1)}, f32[1024]{0:T(1024)}, u32[]{:S(2)}) copy-start(f32[1024]{0:T(1024)} %copy-done.33) | copy-start | bytes 12292
  308.8 13.1 %copy-start.38 = (f32[768]{0:T(1024)S(1)}, f32[768]{0:T(1024)}, u32[]{:S(2)}) copy-start(f32[768]{0:T(1024)} %copy-done.37) | copy-start | bytes 9220
  308.8 13.1 %copy-start.40 = (f32[1024]{0:T(1024)S(1)}, f32[1024]{0:T(1024)}, u32[]{:S(2)}) copy-start(f32[1024]{0:T(1024)} %copy-done.39) | copy-start | bytes 12292
  308.8 13.1 %copy-start.44 = (f32[768]{0:T(1024)S(1)}, f32[768]{0:T(1024)}, u32[]{:S(2)}) copy-start(f32[768]{0:T(1024)} %copy-done.43) | copy-start | bytes 9220
  321.9 11.4 %copy-start.8 = (bf16[1024,12,192]{0,2,1:T(8,128)(2,1)}, bf16[1024,12,192]{0,2,1:T(8,128)(2,1)S(1)}, u32[]{:S(2)}) copy-start(bf16[1024,12,192]{0,2,1:T(8,128)(2,1)S(1)} %bitcast_dynamic-update-slice_fusion) | copy-start | bytes 14155780
  321.9 7.7 copy-start.12
  321.9 7.7 copy-start.22
  321.9 7.7 copy-start.23
  322.0 7.7 copy-start.47
  384.9 9.9 %copy-start.51 = (bf16[768,3072]{1,0:T(8,128)(2,1)S(1)}, bf16[768,3072]{1,0:T(8,128)(2,1)}, u32[]{:S(2)}) copy-start(bf16[768,3072]{1,0:T(8,128)(2,1)} %all-gather.10.cloned.1.call-done) | copy-start | bytes 14155780
  384.9 14.9 %slice-start.6 = ((s8[4718592]{0:T(1024)(128)(4,1)}), s8[4194304]{0:T(1024)(128)(4,1)S(1)}, s32[]{:S(2)}) async-start(s8[4718592]{0:T(1024)(128)(4,1)} %bitcast.166), calls=%async_computation.19 | async-start | bytes 8388608
  399.9 7.5 copy-start.13
  476.4 115.2 %reduce-scatter.5.cloned.1.call-start = ((), (), s32[]{:S(2)}) async-start(), calls=%async_computation.8 | async-start | bytes 7962624 | tf_op jit(solution)/shard_map/reduce_scatter | solution.py:263
  482.7 209.1 %reduce-scatter.11.cloned.1.call-start = ((), (), s32[]{:S(2)}) async-start(), calls=%async_computation.11 | async-start | bytes 10616832 | tf_op jit(solution)/shard_map/reduce_scatter | solution.py:269
  490.8 301.2 %reduce-scatter.9.cloned.1.call-start = ((), (), s32[]{:S(2)}) async-start(), calls=%async_computation.10 | async-start | bytes 10616832 | tf_op jit(solution)/shard_map/reduce_scatter | solution.py:267
  500.0 292.1 %copy-start.36 = (f32[768]{0:T(1024)S(1)}, f32[768]{0:T(1024)}, u32[]{:S(2)}) copy-start(f32[768]{0:T(1024)} %copy-done.35) | copy-start | bytes 9220
  500.0 387.7 %all-reduce.20.cloned.1.call-start = ((), (), s32[]{:S(2)}) async-start(), calls=%async_computation.12 | async-start | bytes 7077888 | tf_op jit(solution)/shard_map/psum | solution.py:272
  829.7 57.9 %copy-start.54 = (f32[96]{0:T(128)}, f32[96]{0:T(128)S(1)}, u32[]{:S(2)}) copy-start(f32[96]{0:T(128)S(1)} %get-tuple-element.143) | copy-start | bytes 1156
  829.7 8.7 copy-start.18
  829.7 8.7 copy-start.53
  (24 other events, 86.8 us)
Sparse Core Ops, SparseCore 0:
  9.6 25.5 all-gather.7
  36.9 41.2 all-gather.5
  79.8 50.0 all-gather.9
  131.4 49.9 all-gather.11
  476.5 36.8 reduce-scatter.6
  515.5 76.0 reduce-scatter.4
  593.9 97.8 reduce-scatter.10
  694.1 97.8 reduce-scatter.8
  795.5 92.0 all-reduce.19
where the time goes:
time: 908 us; the launch traced here: 902 us
  waiting for transfers between devices  332 us (37%)
  matrix products  263 us (29%)
  other arithmetic  125 us (14%)
  blocking collectives  121 us (13%)
  local copies, waits for them, and re-layouts  32.2 us (4%)
  between operations  29.1 us (3%)
    reduce_scatter x1, waiting for transfers between devices, body(): lax.psum_scatter(scaled[8], 'fsdp', scatter_dimension=0, tiled=True)  100 us
    reduce_scatter x1, waiting for transfers between devices, body(): lax.psum_scatter(scaled[10], 'fsdp', scatter_dimension=0, tiled=True)  100 us
    reduce_scatter x1, waiting for transfers between devices, body(): lax.psum_scatter(scaled[4], 'fsdp', scatter_dimension=0, tiled=True)  78.2 us
    unnamed x2, blocking collectives  57.7 us
    psum x1, waiting for transfers between devices, body(): lax.psum((owned[0], owned[1], owned[2], owned[3], owned[4], owned[5], own...  42.2 us
    convert_element_type x1, other arithmetic, body(): score_grad = (probs * (prob_grad - row_dot)).astype(bf16)  42 us
    dot_general x2, matrix products, body(): jnp.einsum('qhd,khd->hqk', head_block, values_all, preferred_element_type...  39.2 us
    psum x1, blocking collectives, body(): lax.psum(jnp.where(mine, squares, jnp.float32(0.0)), ('dp', 'fsdp'))  38.9 us
  transfers between devices with their start and end apart: 9, of which 5 were waited for; matrix products, arithmetic and copies ran while one was open for 39% of the time, Pallas kernels for 0%

commit v1 on v0

v1 whole, which is shorter than its diff:
```python
import functools
import math

import jax
import jax.numpy as jnp
from jax import lax
from jax.experimental import pallas as pl
from jax.experimental.pallas import tpu as pltpu
from jax.sharding import PartitionSpec as P

HEAD_DIM = 64
ROT_DIM = 16
LANES = 128
f32 = jnp.float32
bf16 = jnp.bfloat16
VMEM_LIMIT = 60 * 2**20


def nn(left, right):
    return lax.dot_general(left, right, (((1,), (0,)), ((), ())), preferred_element_type=f32)


def nt(left, right):
    return lax.dot_general(left, right, (((1,), (1,)), ((), ())), preferred_element_type=f32)


def tn(left, right):
    return lax.dot_general(left, right, (((0,), (0,)), ((), ())), preferred_element_type=f32)


def fold(row):
    total = row[:, 0:LANES]
    for start in range(LANES, row.shape[1], LANES):
        total = total + row[:, start : start + LANES]
    return total


def fixed(shape):
    return pl.BlockSpec(shape, lambda *_: (0,) * len(shape), pipeline_mode=pl.Buffered(1))


def params():
    return pltpu.CompilerParams(vmem_limit_bytes=VMEM_LIMIT)


def store_rows(value, coords, keep_ref, send_ref):
    rows = value.shape[0] // 8
    half = rows // 2
    first = coords[0] == 0
    for z in range(4):
        even = value[2 * z * rows : (2 * z + 1) * rows].astype(bf16)
        odd = value[(2 * z + 1) * rows : (2 * z + 2) * rows].astype(bf16)
        kept = jnp.where(first, even, odd)
        sent = jnp.where(first, odd, even)
        for y in range(2):
            for t in range(value.shape[1] // LANES):
                at = (0, y ^ coords[2], z ^ coords[3], t)
                lanes = slice(t * LANES, (t + 1) * LANES)
                keep_ref[at] = kept[y * half : (y + 1) * half, lanes]
                send_ref[at] = sent[y * half : (y + 1) * half, lanes]


def qkv_kernel(x_ref, ln_ref, w_ref, b_ref, c_ref, sa_ref, sb_ref, h1_ref, h2_ref, o_ref):
    x = x_ref[...].astype(f32)
    centred = x - jnp.mean(x, -1, keepdims=True)
    normed = centred * lax.rsqrt(jnp.mean(centred * centred, -1, keepdims=True) + 1e-05)
    h1 = (normed * ln_ref[0:1, :] + ln_ref[1:2, :]).astype(bf16)
    h2_ref[...] = (normed * ln_ref[2:3, :] + ln_ref[3:4, :]).astype(bf16)
    h1_ref[...] = h1
    width = x.shape[1]
    cosine, ahead, behind = c_ref[...], sa_ref[...], sb_ref[...]
    low = lax.broadcasted_iota(jnp.int32, (1, LANES), 1) < HEAD_DIM

    def turn(y):
        return y * cosine - pltpu.roll(y * ahead, LANES - 8, 1) - pltpu.roll(y * behind, 8, 1)

    for part in range(3):
        cols = slice(part * width, (part + 1) * width)
        y = nn(h1, w_ref[:, cols]) + b_ref[:, cols]
        for pair in range(2):
            base = pair * 3 * LANES
            t0 = y[:, base : base + LANES]
            t1 = y[:, base + LANES : base + 2 * LANES]
            t2 = y[:, base + 2 * LANES : base + 3 * LANES]
            queries = turn(jnp.where(low, t0, t1)) * (HEAD_DIM**-0.5)
            keys = turn(pltpu.roll(jnp.where(low, t2, t0), HEAD_DIM, 1))
            at = (2 * part + pair) * LANES
            o_ref[:, at : at + LANES] = queries.astype(bf16)
            o_ref[:, width + at : width + at + LANES] = keys.astype(bf16)
            o_ref[:, 2 * width + at : 2 * width + at + LANES] = jnp.where(low, t1, t2).astype(bf16)


def qkv_forward(x, ln, weight, bias, tables, rows=256):
    count, width = x.shape
    block = lambda n: pl.BlockSpec((rows, n), lambda i: (i, 0))
    return pl.pallas_call(
        qkv_kernel,
        grid=(count // rows,),
        in_specs=[block(width), fixed(ln.shape), fixed(weight.shape), fixed(bias.shape)]
        + [block(LANES)] * 3,
        out_specs=[block(width), block(width), block(3 * width)],
        out_shape=[
            jax.ShapeDtypeStruct((count, width), bf16),
            jax.ShapeDtypeStruct((count, width), bf16),
            jax.ShapeDtypeStruct((count, 3 * width), bf16),
        ],
        compiler_params=params(),
        cost_estimate=pl.CostEstimate(
            flops=6 * count * width * width, bytes_accessed=14 * 2**20, transcendentals=0
        ),
        name="qkv_forward",
    )(x, ln, weight, bias, *tables)


def rotary_tables(count):
    positions = jnp.arange(count).astype(f32)
    inverse = 10000.0 ** (-jnp.arange(0, ROT_DIM, 2).astype(f32) / ROT_DIM)
    angles = positions[:, None] * inverse[None, :]
    cosine, sine = jnp.cos(angles), jnp.sin(angles)
    rest = HEAD_DIM - ROT_DIM
    one, zero, none = jnp.ones((count, rest), f32), jnp.zeros((count, rest), f32), jnp.zeros_like(sine)
    return (
        jnp.concatenate([cosine, cosine, one] * 2, -1),
        jnp.concatenate([none, sine, zero] * 2, -1),
        jnp.concatenate([-sine, none, zero] * 2, -1),
    )


def attention_kernel(
    q_ref, k_ref, v_ref, cot_ref, w_ref, c_ref, sa_ref, sb_ref, a_ref, dqkv_ref, dq, dkt, dvt, *, rows
):
    count = q_ref.shape[0]
    blocks = count // rows
    low = lax.broadcasted_iota(jnp.int32, (1, LANES), 1) < HEAD_DIM
    causal = lax.broadcasted_iota(jnp.int32, (rows, rows), 1) <= lax.broadcasted_iota(
        jnp.int32, (rows, rows), 0
    )

    def unturn(y):
        return (
            y * c_ref[...]
            + pltpu.roll(y * sa_ref[...], LANES - 8, 1)
            + pltpu.roll(y * sb_ref[...], 8, 1)
        )

    for i in reversed(range(blocks)):
        before = rows * i
        here = slice(before, before + rows)
        past = slice(0, before)
        q = q_ref[here, :]
        da = nt(cot_ref[here, :], w_ref[...]).astype(bf16)
        q_turned, da_turned = q.T, da.T
        outs, grads = [], []
        for h in range(2):
            mine = low if h == 0 else jnp.logical_not(low)
            head = slice(HEAD_DIM * h, HEAD_DIM * (h + 1))
            qh = jnp.where(mine, q, jnp.zeros_like(q))
            dah = jnp.where(mine, da, jnp.zeros_like(da))
            s_here = jnp.where(causal, nt(qh, k_ref[here, :]), -1e30)
            highest = jnp.max(s_here, -1, keepdims=True)
            if before:
                s_past = nt(qh, k_ref[past, :])
                highest = jnp.maximum(highest, jnp.max(s_past, -1, keepdims=True))
                e_past = jnp.exp(s_past - highest)
            e_here = jnp.exp(s_here - highest)
            total = jnp.sum(e_here, -1, keepdims=True)
            if before:
                total = total + jnp.sum(e_past, -1, keepdims=True)
            inverse = 1.0 / total
            p_here = e_here * inverse
            l_here = p_here.astype(bf16)
            out = nn(l_here, v_ref[here, :])
            if before:
                p_past = e_past * inverse
                l_past = p_past.astype(bf16)
                out = out + nn(l_past, v_ref[past, :])
            row_dot = jnp.sum(jnp.where(mine, out * dah.astype(f32), 0.0), -1, keepdims=True)
            ds_here = (p_here * (nt(dah, v_ref[here, :]) - row_dot)).astype(bf16)
            grad = nn(ds_here, k_ref[here, :])
            if before:
                ds_past = (p_past * (nt(dah, v_ref[past, :]) - row_dot)).astype(bf16)
                grad = grad + nn(ds_past, k_ref[past, :])
            outs.append(out)
            grads.append(grad)
            qt, dat = q_turned[head, :], da_turned[head, :]
            if i == blocks - 1:
                dkt[head, here] = nn(qt, ds_here)
                dvt[head, here] = nn(dat, l_here)
                if before:
                    dkt[head, past] = nn(qt, ds_past)
                    dvt[head, past] = nn(dat, l_past)
            else:
                dkt[head, here] += nn(qt, ds_here)
                dvt[head, here] += nn(dat, l_here)
                if before:
                    dkt[head, past] += nn(qt, ds_past)
                    dvt[head, past] += nn(dat, l_past)
        a_ref[here, :] = jnp.where(low, outs[0], outs[1]).astype(bf16)
        dq[here, :] = jnp.where(low, grads[0], grads[1]) * (HEAD_DIM**-0.5)
    gq = unturn(dq[...])
    gk = pltpu.roll(unturn(dkt[...].T), HEAD_DIM, 1)
    gv = dvt[...].T
    dqkv_ref[:, 0:LANES] = jnp.where(low, gq, gk).astype(bf16)
    dqkv_ref[:, LANES : 2 * LANES] = jnp.where(low, gv, gq).astype(bf16)
    dqkv_ref[:, 2 * LANES : 3 * LANES] = jnp.where(low, gk, gv).astype(bf16)


def attention(qkv, cot, out_weight, tables, rows=256):
    count, width = cot.shape
    pairs = width // LANES
    column = lambda offset: pl.BlockSpec((count, LANES), lambda p: (0, offset + p))
    return pl.pallas_call(
        functools.partial(attention_kernel, rows=rows),
        grid=(pairs,),
        in_specs=[column(0), column(pairs), column(2 * pairs), fixed((count, width))]
        + [pl.BlockSpec((LANES, width), lambda p: (p, 0))]
        + [fixed((count, LANES))] * 3,
        out_specs=[column(0), pl.BlockSpec((count, 3 * LANES), lambda p: (0, p))],
        out_shape=[
            jax.ShapeDtypeStruct((count, width), bf16),
            jax.ShapeDtypeStruct((count, 3 * width), bf16),
        ],
        scratch_shapes=[
            pltpu.VMEM((count, LANES), f32),
            pltpu.VMEM((LANES, count), f32),
            pltpu.VMEM((LANES, count), f32),
        ],
        compiler_params=params(),
        cost_estimate=pl.CostEstimate(
            flops=30 * 10**9, bytes_accessed=20 * 2**20, transcendentals=8 * 10**6
        ),
        name="attention",
    )(qkv, qkv, qkv, cot, out_weight, *tables)


def feed_kernel(
    co_ref, h2_ref, cot_ref, up_ref, upb_ref, down_ref,
    g_ref, upk_ref, ups_ref, dnk_ref, dns_ref, ubg_ref, dh2_ref, sq_ref,
):
    j = pl.program_id(0)
    u = nn(h2_ref[...], up_ref[...]) + upb_ref[...]
    act = nt(cot_ref[...], down_ref[...])
    cdf = 0.5 * (1.0 + lax.erf(u * math.sqrt(0.5)))
    pdf = jnp.exp(-0.5 * u * u) * (1.0 / math.sqrt(2.0 * math.pi))
    g = (u * cdf).astype(bf16)
    du = (act * (cdf + u * pdf)).astype(bf16)
    g_ref[...] = g
    bias_grad = jnp.sum(du.astype(f32), 0, keepdims=True)
    ubg_ref[...] = bias_grad
    up_grad = tn(h2_ref[...], du)
    down_grad = tn(g, cot_ref[...])
    store_rows(up_grad, co_ref, upk_ref, ups_ref)
    x_mine = co_ref[1]
    for unit in range(2):
        place = 2 * (j % 3) + unit
        core, sub = place // 3, place % 3
        rows = down_grad[unit * LANES : (unit + 1) * LANES].astype(bf16)
        half = LANES // 2

        def put(ref):
            for x in range(2):
                for y in range(2):
                    for t in range(3):
                        lanes = slice((3 * x + t) * LANES, (3 * x + t + 1) * LANES)
                        ref[x ^ x_mine, y ^ co_ref[2], 0, sub, t] = rows[y * half : (y + 1) * half, lanes]

        pl.when(core == co_ref[0])(lambda: put(dnk_ref))
        pl.when(core != co_ref[0])(lambda: put(dns_ref))
    part = nt(du, up_ref[...])

    @pl.when(j == 0)
    def _():
        dh2_ref[...] = part
        sq_ref[...] = jnp.zeros_like(sq_ref)

    @pl.when(j > 0)
    def _():
        dh2_ref[...] += part

    sq_ref[0:1, :] += fold(
        jnp.sum(up_grad * up_grad, 0, keepdims=True) + bias_grad * bias_grad
    ) + fold(jnp.sum(down_grad * down_grad, 0, keepdims=True))


def feed(coords, h2, cot, up, up_bias, down, tile=256):
    count, width = h2.shape
    hidden = up.shape[1]
    per_x = hidden // 2 // tile
    tiles = tile // LANES
    up_piece = jax.ShapeDtypeStruct((2, 2, 4, hidden // 2 // LANES, width // 16, LANES), bf16)
    down_piece = jax.ShapeDtypeStruct((2, 2, 4, 3, width // 2 // LANES, LANES // 2, LANES), bf16)
    up_spec = pl.BlockSpec(
        (1, 2, 4, tiles, width // 16, LANES),
        lambda j, co: ((j // per_x) ^ co[1], 0, 0, j % per_x, 0, 0),
    )
    down_spec = pl.BlockSpec(
        (2, 2, 1) + down_piece.shape[3:], lambda j, co: (0, 0, (j // 3) ^ co[3], 0, 0, 0, 0)
    )
    return pl.pallas_call(
        feed_kernel,
        grid_spec=pltpu.PrefetchScalarGridSpec(
            num_scalar_prefetch=1,
            grid=(hidden // tile,),
            in_specs=[
                fixed((count, width)),
                fixed((count, width)),
                pl.BlockSpec((width, tile), lambda j, co: (0, j)),
                pl.BlockSpec((1, tile), lambda j, co: (0, j)),
                pl.BlockSpec((tile, width), lambda j, co: (j, 0)),
            ],
            out_specs=[
                pl.BlockSpec((count, tile), lambda j, co: (0, j)),
                up_spec,
                up_spec,
                down_spec,
                down_spec,
                pl.BlockSpec((1, tile), lambda j, co: (0, j)),
                pl.BlockSpec((count, width), lambda j, co: (0, 0)),
                pl.BlockSpec((8, LANES), lambda j, co: (0, 0)),
            ],
        ),
        out_shape=[
            jax.ShapeDtypeStruct((count, hidden), bf16),
            up_piece,
            up_piece,
            down_piece,
            down_piece,
            jax.ShapeDtypeStruct((1, hidden), f32),
            jax.ShapeDtypeStruct((count, width), f32),
            jax.ShapeDtypeStruct((8, LANES), f32),
        ],
        compiler_params=params(),
        cost_estimate=pl.CostEstimate(
            flops=10 * count * width * hidden, bytes_accessed=32 * 2**20, transcendentals=8 * 10**6
        ),
        name="feed",
    )(coords, h2, cot, up, up_bias, down)


def grad_kernel(co_ref, left_ref, right_ref, w_ref, keep_ref, send_ref, bias_ref, back_ref, sq_ref):
    j = pl.program_id(0)
    right = right_ref[...]
    grad = tn(left_ref[...], right)
    bias_grad = jnp.sum(right.astype(f32), 0, keepdims=True)
    bias_ref[...] = bias_grad
    store_rows(grad, co_ref, keep_ref, send_ref)
    part = nt(right, w_ref[...])

    @pl.when(j == 0)
    def _():
        back_ref[...] = part
        sq_ref[...] = jnp.zeros_like(sq_ref)

    @pl.when(j > 0)
    def _():
        back_ref[...] += part

    sq_ref[0:1, :] += fold(jnp.sum(grad * grad, 0, keepdims=True) + bias_grad * bias_grad)


def plain_grad_kernel(co_ref, left_ref, right_ref, keep_ref, send_ref, bias_ref, sq_ref):
    right = right_ref[...]
    grad = tn(left_ref[...], right)
    bias_grad = jnp.sum(right.astype(f32), 0, keepdims=True)
    bias_ref[...] = bias_grad
    store_rows(grad, co_ref, keep_ref, send_ref)

    @pl.when(pl.program_id(0) == 0)
    def _():
        sq_ref[...] = jnp.zeros_like(sq_ref)

    sq_ref[0:1, :] += fold(jnp.sum(grad * grad, 0, keepdims=True) + 2.0 * bias_grad * bias_grad)


def weight_grad(coords, left, right, weight=None, tile=384):
    count, width = left.shape
    cols = right.shape[1]
    per_x = cols // 2 // tile
    piece = jax.ShapeDtypeStruct((2, 2, 4, cols // 2 // LANES, width // 16, LANES), bf16)
    spec = pl.BlockSpec(
        (1, 2, 4, tile // LANES, width // 16, LANES),
        lambda j, co: ((j // per_x) ^ co[1], 0, 0, j % per_x, 0, 0),
    )
    back = [] if weight is None else [weight]
    return pl.pallas_call(
        plain_grad_kernel if weight is None else grad_kernel,
        grid_spec=pltpu.PrefetchScalarGridSpec(
            num_scalar_prefetch=1,
            grid=(cols // tile,),
            in_specs=[fixed((count, width)), pl.BlockSpec((count, tile), lambda j, co: (0, j))]
            + [pl.BlockSpec((width, tile), lambda j, co: (0, j))] * len(back),
            out_specs=[spec, spec, pl.BlockSpec((1, tile), lambda j, co: (0, j))]
            + [pl.BlockSpec((count, width), lambda j, co: (0, 0))] * len(back)
            + [pl.BlockSpec((8, LANES), lambda j, co: (0, 0))],
        ),
        out_shape=[piece, piece, jax.ShapeDtypeStruct((1, cols), f32)]
        + [jax.ShapeDtypeStruct((count, width), f32)] * len(back)
        + [jax.ShapeDtypeStruct((8, LANES), f32)],
        compiler_params=params(),
        cost_estimate=pl.CostEstimate(
            flops=2 * (1 + len(back)) * count * width * cols,
            bytes_accessed=16 * 2**20,
            transcendentals=0,
        ),
        name="weight_grad",
    )(coords, left, right, *back)


def norm_back_kernel(x_ref, cot_ref, dh1_ref, dh2_ref, ln_ref, dx_ref, sums_ref):
    x = x_ref[...].astype(f32)
    centred = x - jnp.mean(x, -1, keepdims=True)
    inverse = lax.rsqrt(jnp.mean(centred * centred, -1, keepdims=True) + 1e-05)
    normed = centred * inverse
    dh1, dh2 = dh1_ref[...], dh2_ref[...]
    scaled = dh1 * ln_ref[0:1, :] + dh2 * ln_ref[2:3, :]
    spread = (
        scaled
        - jnp.mean(scaled, -1, keepdims=True)
        - normed * jnp.mean(scaled * normed, -1, keepdims=True)
    )
    dx_ref[...] = cot_ref[...].astype(f32) + inverse * spread

    @pl.when(pl.program_id(0) == 0)
    def _():
        sums_ref[...] = jnp.zeros_like(sums_ref)

    for row, value in enumerate((dh1 * normed, dh1, dh2 * normed, dh2)):
        sums_ref[row : row + 1, :] += jnp.sum(value, 0, keepdims=True)


def norm_back(x, cot, dh1, dh2, ln, rows=256):
    count, width = x.shape
    block = pl.BlockSpec((rows, width), lambda i: (i, 0))
    return pl.pallas_call(
        norm_back_kernel,
        grid=(count // rows,),
        in_specs=[block] * 4 + [fixed(ln.shape)],
        out_specs=[block, pl.BlockSpec((8, width), lambda i: (0, 0))],
        out_shape=[
            jax.ShapeDtypeStruct((count, width), f32),
            jax.ShapeDtypeStruct((8, width), f32),
        ],
        compiler_params=params(),
        cost_estimate=pl.CostEstimate(
            flops=30 * count * width, bytes_accessed=12 * 2**20, transcendentals=0
        ),
        name="norm_back",
    )(x, cot, dh1, dh2, ln)


def body(
    tokens_in, ln1_gain, ln1_bias, ln2_gain, ln2_bias, qkv_weight, qkv_bias, out_weight, out_bias,
    up_weight, up_bias, down_weight, down_bias, cotangent, lengths, assignment, clip_bound,
):
    dp, fsdp = lax.axis_size("dp"), lax.axis_size("fsdp")
    both = ("dp", "fsdp")
    total = dp * fsdp
    fast = (dp, fsdp) == (4, 8)
    me = lax.axis_index("dp") * fsdp + lax.axis_index("fsdp")

    def swap(value, bit):
        return lax.ppermute(value, both, [(i, i ^ bit) for i in range(total)])

    def spread_sum(value, bits):
        for bit in bits:
            value = value + swap(value, bit)
        return value

    smalls = (ln1_gain, ln1_bias, ln2_gain, ln2_bias, qkv_bias, out_bias, up_bias, down_bias)
    packed = jnp.concatenate(smalls)
    if fast:
        slot = lax.broadcasted_iota(jnp.int32, (fsdp, 1), 0) == lax.axis_index("fsdp")
        rows = jnp.where(slot, packed[None, :], jnp.zeros_like(packed)[None, :])
        rows = spread_sum(rows, (1, 2, 4))
    else:
        rows = lax.all_gather(packed, "fsdp", axis=0)
    vectors, start = [], 0
    for entry in smalls:
        stop = start + entry.shape[0]
        vectors.append(rows[:, start:stop].reshape(1, -1).astype(f32))
        start = stop
    ln = jnp.concatenate(vectors[:4] + [jnp.zeros((4, vectors[0].shape[1]), f32)], 0)
    qkv_b, out_b, up_b, down_b = vectors[4:]

    gather = lambda w: lax.all_gather(w, "fsdp", axis=0, tiled=True)
    w_qkv, w_out, w_up, w_down = (gather(w) for w in (qkv_weight, out_weight, up_weight, down_weight))

    if fast:
        coords = jnp.stack([me & 1, (me >> 3) & 1, (me >> 4) & 1, (me >> 1) & 3]).astype(jnp.int32)
    else:
        coords = jnp.zeros((4,), jnp.int32)

    tokens = tokens_in[0]
    count, width = tokens.shape
    valid = lax.broadcasted_iota(jnp.int32, (count, 1), 0) < lengths[0]
    cot = jnp.where(valid, cotangent[0], jnp.zeros_like(cotangent[0]))
    tables = rotary_tables(count)

    h1, h2, qkv = qkv_forward(tokens, ln, w_qkv, qkv_b, tables)
    heads, dqkv = attention(qkv, cot, w_out, tables)
    out_keep, out_send, cot_sum, out_sq = weight_grad(coords, heads, cot)
    qkv_keep, qkv_send, qkv_bias_grad, dh1, qkv_sq = weight_grad(coords, h1, dqkv, w_qkv)
    act, up_keep, up_send, down_keep, down_send, up_bias_grad, dh2, feed_sq = feed(
        coords, h2, cot, w_up, up_b, w_down
    )
    dx, ln_sums = norm_back(tokens, cot, dh1, dh2, ln)
    ln_grads = ln_sums[:4]

    squares = jnp.sum(out_sq + qkv_sq + feed_sq) + jnp.sum(ln_grads * ln_grads)
    mine = jnp.arange(total, dtype=jnp.int32) == assignment[0]
    held = jnp.where(mine, squares, 0.0)
    squares_all = spread_sum(held, (1, 2, 4, 8, 16)) if fast else lax.psum(held, both)
    norms = jnp.sqrt(squares_all)
    order = jnp.arange(total)
    ahead = (norms[None, :] < norms[:, None]) | (
        (norms[None, :] == norms[:, None]) & (order[None, :] < order[:, None])
    )
    rank = jnp.sum(ahead.astype(jnp.int32), 1)
    median = jnp.sum(jnp.where(rank == total // 2, norms, 0.0))
    bound = median * clip_bound[0].astype(f32) / 8.0
    clip_scale = jnp.minimum(1.0, bound / (norms + 1e-06))
    own = jnp.sum(jnp.where(mine, clip_scale, 0.0))
    share = own / total

    mixed = (
        tokens.astype(f32)
        + (nn(heads, w_out) + out_b)
        + (nn(act, w_down) + down_b)
    )
    mixed = jnp.where(valid, mixed, 0.0).astype(bf16)[None]
    tokens_grad = (own * dx).astype(bf16)[None]

    small_grads = jnp.concatenate(
        [ln_grads.reshape(-1), qkv_bias_grad[0], cot_sum[0], up_bias_grad[0]]
    ).reshape(-1, LANES)
    small_grads = small_grads * share
    small_grads = spread_sum(small_grads, (1, 2, 4, 8, 16)) if fast else lax.psum(small_grads, both)
    small_grads = small_grads.reshape(-1)

    def part(first, length):
        piece = small_grads[first : first + length].reshape(fsdp, length // fsdp)
        return lax.dynamic_index_in_dim(piece, lax.axis_index("fsdp"), 0, keepdims=False)

    offsets = [(i * width, width) for i in range(4)]
    offsets += [(4 * width, 3 * width), (7 * width, width), (8 * width, up_b.shape[1])]
    g1, b1, g2, b2, gqb, gob, gub = (part(*o) for o in offsets)

    pieces = (
        (qkv_keep, qkv_send), (out_keep, out_send), (up_keep, up_send), (down_keep, down_send)
    )

    if fast:
        other = jnp.sum(jnp.where(jnp.arange(total) == swap(assignment, 1)[0], clip_scale, 0.0)) / total
        finals = []
        for keep, send in pieces:
            recv = swap(send, 1)
            add = lambda a, b: (a.astype(f32) + b.astype(f32)).astype(bf16)
            summed = lambda at: (share * keep[at].astype(f32) + other * recv[at].astype(f32)).astype(bf16)
            near, far = slice(0, 2), slice(2, 4)
            near_sum = add(summed((0, slice(None), near)), swap(summed((1, slice(None), near)), 8))
            far_sum = add(summed((slice(None), 0, far)), swap(summed((slice(None), 1, far)), 16))
            near_sum = add(near_sum[0], swap(near_sum[1], 16))
            far_sum = add(far_sum[0], swap(far_sum[1], 8))
            line = add(near_sum, swap(far_sum, 4))
            line = add(line[0], swap(line[1], 2))
            row = jnp.stack([line, swap(line, 8)])
            finals.append(jnp.stack([row, swap(row, 16)], 1))
        x_mine, y_mine = coords[1], coords[2]
        outs = []
        for piece in finals:
            piece = jnp.where(x_mine == 0, piece, piece[::-1])
            piece = jnp.where(y_mine == 0, piece, piece[:, ::-1])
            outs.append(piece.astype(f32))
        gq, go, gu = (
            p.transpose(1, 3, 0, 2, 4).reshape(2 * p.shape[3], -1) for p in outs[:3]
        )
        gd = outs[3].transpose(2, 1, 4, 0, 3, 5).reshape(-1, width)
    else:
        outs = []
        for keep, send in pieces[:3]:
            whole = jnp.stack([keep, send])
            whole = whole.transpose(3, 0, 2, 5, 1, 4, 6).reshape(width, -1)
            outs.append((whole.astype(f32) * share).astype(bf16))
        whole = jnp.stack(pieces[3])
        whole = whole.transpose(3, 0, 4, 2, 6, 1, 5, 7).reshape(-1, width)
        outs.append((whole.astype(f32) * share).astype(bf16))
        gq, go, gu, gd = (
            lax.psum(
                lax.psum_scatter(w, "fsdp", scatter_dimension=0, tiled=True).astype(f32), "dp"
            )
            for w in outs
        )
    return (mixed, tokens_grad, clip_scale, g1, b1, g2, b2, gq, gqb, go, gob, gu, gub, gd, gob)


def solution(mesh):
    rows, cols, flat = P("fsdp", None), P("fsdp"), P(("dp", "fsdp"))
    slots = P(("dp", "fsdp"), None, None)
    return jax.shard_map(
        body,
        mesh=mesh,
        in_specs=(slots, cols, cols, cols, cols, rows, cols, rows, cols, rows, cols, rows, cols)
        + (slots, flat, flat, P()),
        out_specs=(slots, slots, P(), cols, cols, cols, cols, rows, cols, rows, cols, rows, cols)
        + (rows, cols),
        check_vma=False,
    )
```

time: 908 us -> 418 us (0.46)
  matrix products: 263 us -> 11.6 us
  waiting for transfers between devices: 332 us -> 147 us
  Pallas kernels: 0 us -> 136 us
  blocking collectives: 121 us -> 0 us
  other arithmetic: 125 us -> 30.8 us
  starting transfers between devices: 0.36 us -> 49.6 us
  local copies, waits for them, and re-layouts: 32.2 us -> 19.1 us
    reduce_scatter x4 -> x0, waiting for transfers between devices: 287 us -> none  [the longest x1 100 us: body(): lax.psum_scatter(scaled[8], 'fsdp', scatter_dimension=0, tiled=True)]
    dot_general x24 -> x2, matrix products: 263 us -> 11.6 us  [nn(): lax.dot_general(left, right, (((1,), (0,)), ((), ())), preferred_element_...]
    pallas_call x0 -> x6, Pallas kernels: none -> 136 us  [the longest x1 49.5 us: attention(): pl.pallas_call(functools.partial(attention_kernel, rows=rows), grid=(pair...]
    ppermute x0 -> x50, waiting for transfers between devices: none -> 78.9 us  [swap(): return lax.ppermute(value, both, [(i, i ^ bit) for i in range(total)])]
    all_gather x4, waiting for transfers between devices: 0.01 us -> 65.6 us  [body(): gather = lambda w: lax.all_gather(w, 'fsdp', axis=0, tiled=True)]
    unnamed x2 -> x0, blocking collectives: 57.7 us -> none
    psum x2 -> x0, blocking collectives: 49.5 us -> none  [the longest x1 38.9 us: body(): lax.psum(jnp.where(mine, squares, jnp.float32(0.0)), ('dp', 'fsdp'))]
    ppermute x0 -> x50, starting transfers between devices: none -> 49.4 us  [swap(): return lax.ppermute(value, both, [(i, i ^ bit) for i in range(total)])]
  transfers between devices with their start and end apart: 9 -> 54, of which waited for: 5 -> 31; matrix products, arithmetic and copies ran while one was open for 39% -> 14% of each run, Pallas kernels for 0% -> 33%
where the time goes in v1:
time: 418 us; the launch traced here: 414 us
  waiting for transfers between devices  147 us (35%)
  Pallas kernels  136 us (33%)
  starting transfers between devices  49.6 us (12%)
  other arithmetic  30.8 us (7%)
  between operations  20.3 us (5%)
  local copies, waits for them, and re-layouts  19.1 us (5%)
  matrix products  11.6 us (3%)
    ppermute x50, waiting for transfers between devices, swap(): return lax.ppermute(value, both, [(i, i ^ bit) for i in range(total)])  78.9 us
    all_gather x4, waiting for transfers between devices, body(): gather = lambda w: lax.all_gather(w, 'fsdp', axis=0, tiled=True)  65.6 us
    pallas_call x1, Pallas kernels, attention(): pl.pallas_call(functools.partial(attention_kernel, rows=rows), grid=(pair...  49.5 us
    ppermute x50, starting transfers between devices, swap(): return lax.ppermute(value, both, [(i, i ^ bit) for i in range(total)])  49.4 us
    pallas_call x1, Pallas kernels, feed(): pl.pallas_call(feed_kernel, grid_spec=pltpu.PrefetchScalarGridSpec(num_sc...  45.2 us
    pallas_call x2, Pallas kernels, weight_grad(): pl.pallas_call(plain_grad_kernel if weight is None else grad_kernel, grid...  24 us
    dot_general x2, matrix products, nn(): lax.dot_general(left, right, (((1,), (0,)), ((), ())), preferred_element_...  11.6 us
    pallas_call x1, Pallas kernels, qkv_forward(): pl.pallas_call(qkv_kernel, grid=(count // rows,), in_specs=[block(width),...  10.3 us
  transfers between devices with their start and end apart: 54, of which 31 were waited for; matrix products, arithmetic and copies ran while one was open for 14% of the time, Pallas kernels for 33%

profile of v1, /device:TPU:0, one launch (start us, length us, event | category | flops | bytes accessed | tf_op | source)
XLA Modules:
  0.0 414.5 jit_solution(10701190872899194521)
XLA Ops:
  13.0 3.0 collective-permute-start.1
  16.0 1.9 fusion.39
  18.0 2.9 collective-permute-start.2
  22.2 1.9 concatenate.21.sa_ref
  24.2 1.7 concatenate.22.sb_ref
  26.6 1.7 concatenate.20.c_ref
  30.9 23.1 %all-gather.5.cloned.1.call-done.w_ref = bf16[768,2304]{1,0:T(8,128)(2,1)} async-done(((bf16[96,2304]{1,0:T(8,128)(2,1)}), bf16[768,2304]{1,0:T(8,128)(2,1)}) %all-gather.5.cloned.1.call-update) | async-done | bytes 3538960 | tf_op jit(solution)/shard_map/all_gather | solution.py:485
  54.0 10.3 %qkv_forward.1 = (bf16[1024,768]{1,0:T(8,128)(2,1)}, bf16[1024,768]{1,0:T(8,128)(2,1)}, bf16[1024,2304]{1,0:T(8,128)(2,1)}) custom-call(bf16[1024,768]{1,0:T(8,128)(2,1)} %bitcast.278, f32[8,768]{1,0:T(8,128)} %concatenate.19.ln_ref, bf16[768,2304]{1,0:T(8,128)(2,1)} %all-gather.5.cloned.1.call-done.w_ref, f32[1,2304]{1,0:T(1,128)} %reshape.404.b_ref, ...), custom_call_target="tpu_custom_call" | custom-call | flops 3623878656 | bytes 14680064 | tf_op jit(solution)/shard_map/qkv_forward/pallas_call | solution.py:96
  64.3 13.3 %all-gather.7.cloned.1.call-done.w_ref = bf16[768,768]{1,0:T(8,128)(2,1)} async-done(((bf16[96,768]{1,0:T(8,128)(2,1)}), bf16[768,768]{1,0:T(8,128)(2,1)}) %all-gather.7.cloned.1.call-update) | async-done | bytes 1179664 | tf_op jit(solution)/shard_map/all_gather | solution.py:485
  77.6 49.5 %attention.1 = (bf16[1024,768]{1,0:T(8,128)(2,1)}, bf16[1024,2304]{1,0:T(8,128)(2,1)}) custom-call(bf16[1024,2304]{1,0:T(8,128)(2,1)} %get-tuple-element.39.q_ref.k_ref.v_ref, bf16[1024,2304]{1,0:T(8,128)(2,1)} %get-tuple-element.39.q_ref.k_ref.v_ref, bf16[1024,2304]{1,0:T(8,128)(2,1)} %get-tuple-element.39.q_ref.k_ref.v_ref, ...), custom_call_target="tpu_custom_call" | custom-call | flops 30000001024 | bytes 20971520 | tf_op jit(solution)/shard_map/attention/pallas_call | solution.py:212
  127.1 5.4 %weight_grad.2 = (bf16[2,2,4,3,48,128]{5,4,3,2,1,0:T(8,128)(2,1)}, bf16[2,2,4,3,48,128]{5,4,3,2,1,0:T(8,128)(2,1)}, f32[1,768]{1,0:T(1,128)}, f32[8,128]{1,0:T(8,128)}) custom-call(s32[4]{0:T(128)} %pad_add_fusion.co_ref, bf16[1024,768]{1,0:T(8,128)(2,1)} %get-tuple-element.40.left_ref, bf16[1024,768]{1,0:T(8,128)(2,1)} %bitcast_select_fusion.cot_ref.right_ref), custom_call_target="tpu_custom_call" | custom-call | flops 1207959552 | bytes 16777216 | tf_op jit(solution)/shard_map/weight_grad/pallas_call | solution.py:385
  132.7 18.7 %weight_grad.3 = (bf16[2,2,4,9,48,128]{5,4,3,2,1,0:T(8,128)(2,1)}, bf16[2,2,4,9,48,128]{5,4,3,2,1,0:T(8,128)(2,1)}, f32[1,2304]{1,0:T(1,128)}, f32[1024,768]{1,0:T(8,128)}, f32[8,128]{1,0:T(8,128)}) custom-call(s32[4]{0:T(128)} %pad_add_fusion.co_ref, bf16[1024,768]{1,0:T(8,128)(2,1)} %get-tuple-element.44.left_ref, ...), custom_call_target="tpu_custom_call" | custom-call | flops 7247757312 | bytes 16777216 | tf_op jit(solution)/shard_map/weight_grad/pallas_call | solution.py:385
  152.5 29.1 %all-gather.9.cloned.1.call-done.up_ref = bf16[768,3072]{1,0:T(8,128)(2,1)} async-done(((bf16[96,3072]{1,0:T(8,128)(2,1)}), bf16[768,3072]{1,0:T(8,128)(2,1)}) %all-gather.9.cloned.1.call-update) | async-done | bytes 4718608 | tf_op jit(solution)/shard_map/all_gather | solution.py:485
  181.6 45.2 %feed.1 = (bf16[1024,3072]{1,0:T(8,128)(2,1)}, bf16[2,2,4,12,48,128]{5,4,3,2,1,0:T(8,128)(2,1)}, bf16[2,2,4,12,48,128]{5,4,3,2,1,0:T(8,128)(2,1)}, bf16[2,2,4,3,...) custom-call(s32[4]{0:T(128)} %pad_add_fusion.co_ref, ...), custom_call_target="tpu_custom_call" | custom-call | flops 24159191040 | bytes 33554432 | tf_op jit(solution)/shard_map/feed/pallas_call | solution.py:299
  226.9 6.9 %norm_back.1 = (f32[1024,768]{1,0:T(8,128)}, f32[8,768]{1,0:T(8,128)}) custom-call(bf16[1024,768]{1,0:T(8,128)(2,1)} %bitcast.279, bf16[1024,768]{1,0:T(8,128)(2,1)} %bitcast_select_fusion.cot_ref.right_ref, f32[1024,768]{1,0:T(8,128)} %get-tuple-element.48.dh1_ref, f32[1024,768]{1,0:T(8,128)} %get-tuple-element.49.dh2_ref, f32[8,768]{1,0:T(8,128)} %concatenate.19.ln_ref), custom_call_target="tpu_custom_call" | custom-call | flops 23592960 | bytes 12582912 | tf_op jit(solution)/shard_map/norm_back/pallas_call | solution.py:434
  238.6 3.3 collective-permute-done.4
  243.1 8.9 %fusion.67 = f32[1024,768]{1,0:T(8,128)S(1)} fusion(bf16[1024,3072]{1,0:T(8,128)(2,1)} %get-tuple-element.42, bf16[3072,768]{1,0:T(8,128)(2,1)} %all-gather.11.cloned.1.call-done.down_ref), kind=kOutput, calls=%fused_computation.192 | convolution fusion | flops 4831838208 | bytes 14155776 | tf_op jit(solution)/shard_map/dot_general | solution.py:20
  252.1 1.5 collective-permute-start.6
  253.6 2.7 fusion
  257.9 2.1 collective-permute-done.7
  261.4 1.7 fusion.60
  265.5 1.5 collective-permute-start.26
  267.4 2.2 fusion.1
  273.2 2.3 collective-permute-done.9
  275.5 1.9 collective-permute-start.10
  278.5 2.2 collective-permute-done.10
  287.8 3.8 collective-permute-done.12
  292.5 1.6 collective-permute-start.28
  294.6 1.7 collective-permute-done.25
  299.9 3.3 collective-permute-done.29
  306.1 1.7 fusion.11
  309.3 4.6 %collective-permute-done.18 = bf16[2,9,48,128]{3,2,1,0:T(8,128)(2,1)S(1)} collective-permute-done((bf16[2,9,48,128]{3,2,1,0:T(8,128)(2,1)S(1)}, bf16[2,9,48,128]{3,2,1,0:T(8,128)(2,1)S(1)}, u32[]{:S(2)}, u32[]{:S(2)}) %collective-permute-start.18) | collective-permute-done | bytes 221216 | tf_op jit(solution)/shard_map/ppermute | solution.py:462
  313.9 1.6 collective-permute-start.19
  317.5 5.6 %collective-permute-done.19 = bf16[2,9,48,128]{3,2,1,0:T(8,128)(2,1)S(1)} collective-permute-done((bf16[2,9,48,128]{3,2,1,0:T(8,128)(2,1)S(1)}, bf16[2,9,48,128]{3,2,1,0:T(8,128)(2,1)S(1)}, u32[]{:S(2)}, u32[]{:S(2)}) %collective-permute-start.19) | collective-permute-done | bytes 221216 | tf_op jit(solution)/shard_map/ppermute | solution.py:462
  323.3 4.7 %collective-permute-done.20 = bf16[9,48,128]{2,1,0:T(8,128)(2,1)S(1)} collective-permute-done((bf16[9,48,128]{2,1,0:T(8,128)(2,1)S(1)}, bf16[9,48,128]{2,1,0:T(8,128)(2,1)S(1)}, u32[]{:S(2)}, u32[]{:S(2)}) %collective-permute-start.20) | collective-permute-done | bytes 110624 | tf_op jit(solution)/shard_map/ppermute | solution.py:462
  329.3 3.5 collective-permute-done.21
  334.0 7.2 %collective-permute-done.22 = bf16[2,9,48,128]{3,2,1,0:T(8,128)(2,1)S(1)} collective-permute-done((bf16[2,9,48,128]{3,2,1,0:T(8,128)(2,1)S(1)}, bf16[2,9,48,128]{3,2,1,0:T(8,128)(2,1)S(1)}, u32[]{:S(2)}, u32[]{:S(2)}) %collective-permute-start.22) | collective-permute-done | bytes 221216 | tf_op jit(solution)/shard_map/ppermute | solution.py:462
  347.0 1.8 collective-permute-start.35
  350.9 7.6 %collective-permute-done.44 = bf16[2,2,3,3,64,128]{5,4,3,2,1,0:T(8,128)(2,1)S(1)} collective-permute-done((bf16[2,2,3,3,64,128]{5,4,3,2,1,0:T(8,128)(2,1)S(1)}, bf16[2,2,3,3,64,128]{5,4,3,2,1,0:T(8,128)(2,1)S(1)}, u32[]{:S(2)}, u32[]{:S(2)}) %collective-permute-start.44) | collective-permute-done | bytes 589856 | tf_op jit(solution)/shard_map/ppermute | solution.py:462
  358.9 2.0 fusion.3
  362.2 2.7 collective-permute-start.43
  364.8 2.2 collective-permute-done.35
  367.0 1.9 fusion.5
  371.6 5.6 %collective-permute-done.36 = bf16[2,12,48,128]{3,2,1,0:T(8,128)(2,1)S(1)} collective-permute-done((bf16[2,12,48,128]{3,2,1,0:T(8,128)(2,1)S(1)}, bf16[2,12,48,128]{3,2,1,0:T(8,128)(2,1)S(1)}, u32[]{:S(2)}, u32[]{:S(2)}) %collective-permute-start.36) | collective-permute-done | bytes 294944 | tf_op jit(solution)/shard_map/ppermute | solution.py:462
  377.4 3.5 collective-permute-done.46
  381.1 2.6 collective-permute-start.47
  383.7 3.9 collective-permute-done.37
  390.2 2.8 collective-permute-done.38
  (248 shorter events, 73.4 us)
Async XLA Ops:
  7.3 46.7 %all-gather.5.cloned.1.call-start = ((), (), s32[]{:S(2)}) async-start(), calls=%async_computation | async-start | bytes 3981312 | tf_op jit(solution)/shard_map/all_gather | solution.py:485
  8.0 69.6 %all-gather.7.cloned.1.call-start = ((), (), s32[]{:S(2)}) async-start(), calls=%async_computation.1 | async-start | bytes 1327104 | tf_op jit(solution)/shard_map/all_gather | solution.py:485
  8.8 143.8 %all-gather.11.cloned.1.call-start = ((), (), s32[]{:S(2)}) async-start(), calls=%async_computation.3 | async-start | bytes 5308416 | tf_op jit(solution)/shard_map/all_gather | solution.py:485
  9.5 172.1 %all-gather.9.cloned.1.call-start = ((), (), s32[]{:S(2)}) async-start(), calls=%async_computation.2 | async-start | bytes 5308416 | tf_op jit(solution)/shard_map/all_gather | solution.py:485
  10.8 250.6 %collective-permute-start.13 = (s32[1]{0:T(128)}, s32[1]{0:T(128)}, u32[]{:S(2)}, u32[]{:S(2)}) collective-permute-start(s32[1]{0:T(128)} %param.32), channel_id=1, source_target_pairs={{0,1},{1,0},{2,3},{3,2},{4,5},{5,4},{6,7},{7,6},{8,9},{9,8},{10,11... | collective-permute-start | bytes 20 | tf_op jit(solution)/shard_map/ppermute | solution.py:462
  13.0 4.9 %collective-permute-start.1 = (bf16[8,1248]{1,0:T(8,128)(2,1)S(1)}, bf16[8,1248]{1,0:T(8,128)(2,1)S(1)}, u32[]{:S(2)}, u32[]{:S(2)}) collective-permute-start(bf16[8,1248]{1,0:T(8,128)(2,1)S(1)} %fusion.52), channel_id=1, source_target_pairs={{0,2},{1,3},{2,0},{3,1},{4,6},{5,7},{6,4},{7,5},{8,10},{9,11},{10,... | collective-permute-start | bytes 59912 | tf_op jit(solution)/shard_map/ppermute | solution.py:462
  18.0 10.3 %collective-permute-start.2 = (bf16[8,1248]{1,0:T(8,128)(2,1)S(1)}, bf16[8,1248]{1,0:T(8,128)(2,1)S(1)}, u32[]{:S(2)}, u32[]{:S(2)}) collective-permute-start(bf16[8,1248]{1,0:T(8,128)(2,1)S(1)} %fusion.74), channel_id=1, source_target_pairs={{0,4},{1,5},{2,6},{3,7},{4,0},{5,1},{6,2},{7,3},{8,12},{9,13},{10,... | collective-permute-start | bytes 59912 | tf_op jit(solution)/shard_map/ppermute | solution.py:462
  132.4 132.0 %collective-permute-start.23 = (bf16[2,2,4,3,48,128]{5,4,3,2,1,0:T(8,128)(2,1)}, bf16[2,2,4,3,48,128]{5,4,3,2,1,0:T(8,128)(2,1)}, u32[]{:S(2)}, u32[]{:S(2)}) collective-permute-start(bf16[2,2,4,3,48,128]{5,4,3,2,1,0:T(8,128)(2,1)} %get-tuple-element.58), channel_id=1, source_target_pairs={{0,1},{1,0},{2,3},{3,2},{4,5},{5,4},{6,7},{7,6},{8,9},{9,8},{10,11... | collective-permute-start | bytes 1769480 | tf_op jit(solution)/shard_map/ppermute | solution.py:462
  151.4 120.0 %collective-permute-start.14 = (bf16[2,2,4,9,48,128]{5,4,3,2,1,0:T(8,128)(2,1)}, bf16[2,2,4,9,48,128]{5,4,3,2,1,0:T(8,128)(2,1)}, u32[]{:S(2)}, u32[]{:S(2)}) collective-permute-start(bf16[2,2,4,9,48,128]{5,4,3,2,1,0:T(8,128)(2,1)} %get-tuple-element.56), channel_id=1, source_target_pairs={{0,1},{1,0},{2,3},{3,2},{4,5},{5,4},{6,7},{7,6},{8,9},{9,8},{10,11... | collective-permute-start | bytes 5308424 | tf_op jit(solution)/shard_map/ppermute | solution.py:462
  238.4 102.9 %collective-permute-start.41 = (bf16[2,2,4,3,3,64,128]{6,5,4,3,2,1,0:T(8,128)(2,1)}, bf16[2,2,4,3,3,64,128]{6,5,4,3,2,1,0:T(8,128)(2,1)}, u32[]{:S(2)}, u32[]{:S(2)}) collective-permute-start(bf16[2,2,4,3,3,64,128]{6,5,4,3,2,1,0:T(8,128)(2,1)} %get-tuple-element.62), channel_id=1, source_target_pairs={{0,1},{1,0},{2,3},{3,2},{4,5},{5,4},{6,7},{7,6},{8,9},{9,8},{10,11... | collective-permute-start | bytes 7077896 | tf_op jit(solution)/shard_map/ppermute | solution.py:462
  241.9 10.1 %collective-permute-start.5 = (f32[32]{0:T(128)S(1)}, f32[32]{0:T(128)S(1)}, u32[]{:S(2)}, u32[]{:S(2)}) collective-permute-start(f32[32]{0:T(128)S(1)} %fusion.84), channel_id=1, source_target_pairs={{0,4},{1,5},{2,6},{3,7},{4,0},{5,1},{6,2},{7,3},{8,12},{9,13},{10,... | collective-permute-start | bytes 392 | tf_op jit(solution)/shard_map/ppermute | solution.py:462
  252.1 4.3 %collective-permute-start.6 = (f32[32]{0:T(128)S(1)}, f32[32]{0:T(128)S(1)}, u32[]{:S(2)}, u32[]{:S(2)}) collective-permute-start(f32[32]{0:T(128)S(1)} %add.242), channel_id=1, source_target_pairs={{0,8},{1,9},{2,10},{3,11},{4,12},{5,13},{6,14},{7,15},{8,0},{9,1},... | collective-permute-start | bytes 392 | tf_op jit(solution)/shard_map/ppermute | solution.py:462
  259.9 85.7 %collective-permute-start.32 = (bf16[2,2,4,12,48,128]{5,4,3,2,1,0:T(8,128)(2,1)}, bf16[2,2,4,12,48,128]{5,4,3,2,1,0:T(8,128)(2,1)}, u32[]{:S(2)}, u32[]{:S(2)}) collective-permute-start(bf16[2,2,4,12,48,128]{5,4,3,2,1,0:T(8,128)(2,1)} %get-tuple-element.60), channel_id=1, source_target_pairs={{0,1},{1,0},{2,3},{3,2},{4,5},{5,4},{6,7},{7,6},{8,9},{9,8},{10,11... | collective-permute-start | bytes 7077896 | tf_op jit(solution)/shard_map/ppermute | solution.py:462
  265.5 15.8 %collective-permute-start.26 = (bf16[2,2,3,48,128]{4,3,2,1,0:T(8,128)(2,1)S(1)}, bf16[2,2,3,48,128]{4,3,2,1,0:T(8,128)(2,1)S(1)}, u32[]{:S(2)}, u32[]{:S(2)}) collective-permute-start(bf16[2,2,3,48,128]{4,3,2,1,0:T(8,128)(2,1)S(1)} %fusion.43), channel_id=1, source_target_pairs={{0,16},{1,17},{2,18},{3,19},{4,20},{5,21},{6,22},{7,23},{8,24},{9,... | collective-permute-start | bytes 442376 | tf_op jit(solution)/shard_map/ppermute | solution.py:462
  270.5 12.0 %collective-permute-start.24 = (bf16[2,2,3,48,128]{4,3,2,1,0:T(8,128)(2,1)S(1)}, bf16[2,2,3,48,128]{4,3,2,1,0:T(8,128)(2,1)S(1)}, u32[]{:S(2)}, u32[]{:S(2)}) collective-permute-start(bf16[2,2,3,48,128]{4,3,2,1,0:T(8,128)(2,1)S(1)} %fusion.41), channel_id=1, source_target_pairs={{0,8},{1,9},{2,10},{3,11},{4,12},{5,13},{6,14},{7,15},{8,0},{9,1},... | collective-permute-start | bytes 442376 | tf_op jit(solution)/shard_map/ppermute | solution.py:462
  271.4 4.0 collective-permute-start.9
  275.5 5.2 %collective-permute-start.10 = (f32[72,128]{1,0:T(8,128)S(1)}, f32[72,128]{1,0:T(8,128)S(1)}, u32[]{:S(2)}, u32[]{:S(2)}) collective-permute-start(f32[72,128]{1,0:T(8,128)S(1)} %fusion.83), channel_id=1, source_target_pairs={{0,4},{1,5},{2,6},{3,7},{4,0},{5,1},{6,2},{7,3},{8,12},{9,13},{10,... | collective-permute-start | bytes 110600 | tf_op jit(solution)/shard_map/ppermute | solution.py:462
  280.7 23.9 %collective-permute-start.17 = (bf16[2,2,9,48,128]{4,3,2,1,0:T(8,128)(2,1)S(1)}, bf16[2,2,9,48,128]{4,3,2,1,0:T(8,128)(2,1)S(1)}, u32[]{:S(2)}, u32[]{:S(2)}) collective-permute-start(bf16[2,2,9,48,128]{4,3,2,1,0:T(8,128)(2,1)S(1)} %fusion.29), channel_id=1, source_target_pairs={{0,16},{1,17},{2,18},{3,19},{4,20},{5,21},{6,22},{7,23},{8,24},{9,... | collective-permute-start | bytes 1327112 | tf_op jit(solution)/shard_map/ppermute | solution.py:462
  281.3 4.4 %collective-permute-start.11 = (f32[72,128]{1,0:T(8,128)S(1)}, f32[72,128]{1,0:T(8,128)S(1)}, u32[]{:S(2)}, u32[]{:S(2)}) collective-permute-start(f32[72,128]{1,0:T(8,128)S(1)} %add.249), channel_id=1, source_target_pairs={{0,8},{1,9},{2,10},{3,11},{4,12},{5,13},{6,14},{7,15},{8,0},{9,1},... | collective-permute-start | bytes 110600 | tf_op jit(solution)/shard_map/ppermute | solution.py:462
  284.3 8.2 %collective-permute-start.27 = (bf16[2,3,48,128]{3,2,1,0:T(8,128)(2,1)}, bf16[2,3,48,128]{3,2,1,0:T(8,128)(2,1)S(1)}, u32[]{:S(2)}, u32[]{:S(2)}) collective-permute-start(bf16[2,3,48,128]{3,2,1,0:T(8,128)(2,1)} %slice_bitcast_fusion.22), channel_id=1, source_target_pairs={{0,8},{1,9},{2,10},{3,11},{4,12},{5,13},{6,14},{7,15},{8,0},{9,1},... | collective-permute-start | bytes 221192 | tf_op jit(solution)/shard_map/ppermute | solution.py:462
  285.7 5.9 %collective-permute-start.12 = (f32[72,128]{1,0:T(8,128)S(1)}, f32[72,128]{1,0:T(8,128)S(1)}, u32[]{:S(2)}, u32[]{:S(2)}) collective-permute-start(f32[72,128]{1,0:T(8,128)S(1)} %add.250), channel_id=1, source_target_pairs={{0,16},{1,17},{2,18},{3,19},{4,20},{5,21},{6,22},{7,23},{8,24},{9,... | collective-permute-start | bytes 110600 | tf_op jit(solution)/shard_map/ppermute | solution.py:462
  291.6 4.7 %collective-permute-start.25 = (bf16[2,3,48,128]{3,2,1,0:T(8,128)(2,1)}, bf16[2,3,48,128]{3,2,1,0:T(8,128)(2,1)}, u32[]{:S(2)}, u32[]{:S(2)}) collective-permute-start(bf16[2,3,48,128]{3,2,1,0:T(8,128)(2,1)} %slice_bitcast_fusion.24), channel_id=1, source_target_pairs={{0,16},{1,17},{2,18},{3,19},{4,20},{5,21},{6,22},{7,23},{8,24},{9,... | collective-permute-start | bytes 221192 | tf_op jit(solution)/shard_map/ppermute | solution.py:462
  292.5 5.8 %collective-permute-start.28 = (bf16[2,3,48,128]{3,2,1,0:T(8,128)(2,1)S(1)}, bf16[2,3,48,128]{3,2,1,0:T(8,128)(2,1)S(1)}, u32[]{:S(2)}, u32[]{:S(2)}) collective-permute-start(bf16[2,3,48,128]{3,2,1,0:T(8,128)(2,1)S(1)} %fusion.44), channel_id=1, source_target_pairs={{0,4},{1,5},{2,6},{3,7},{4,0},{5,1},{6,2},{7,3},{8,12},{9,13},{10,... | collective-permute-start | bytes 221192 | tf_op jit(solution)/shard_map/ppermute | solution.py:462
  296.3 9.8 %collective-permute-start.15 = (bf16[2,2,9,48,128]{4,3,2,1,0:T(8,128)(2,1)S(1)}, bf16[2,2,9,48,128]{4,3,2,1,0:T(8,128)(2,1)}, u32[]{:S(2)}, u32[]{:S(2)}) collective-permute-start(bf16[2,2,9,48,128]{4,3,2,1,0:T(8,128)(2,1)S(1)} %fusion.27), channel_id=1, source_target_pairs={{0,8},{1,9},{2,10},{3,11},{4,12},{5,13},{6,14},{7,15},{8,0},{9,1},... | collective-permute-start | bytes 1327112 | tf_op jit(solution)/shard_map/ppermute | solution.py:462
  303.3 13.5 %collective-permute-start.30 = (bf16[3,48,128]{2,1,0:T(8,128)(2,1)S(1)}, bf16[3,48,128]{2,1,0:T(8,128)(2,1)S(1)}, u32[]{:S(2)}, u32[]{:S(2)}) collective-permute-start(bf16[3,48,128]{2,1,0:T(8,128)(2,1)S(1)} %fusion.46), channel_id=1, source_target_pairs={{0,8},{1,9},{2,10},{3,11},{4,12},{5,13},{6,14},{7,15},{8,0},{9,1},... | collective-permute-start | bytes 110600 | tf_op jit(solution)/shard_map/ppermute | solution.py:462
  307.9 6.0 %collective-permute-start.18 = (bf16[2,9,48,128]{3,2,1,0:T(8,128)(2,1)S(1)}, bf16[2,9,48,128]{3,2,1,0:T(8,128)(2,1)S(1)}, u32[]{:S(2)}, u32[]{:S(2)}) collective-permute-start(bf16[2,9,48,128]{3,2,1,0:T(8,128)(2,1)S(1)} %slice_bitcast_fusion.11), channel_id=1, source_target_pairs={{0,8},{1,9},{2,10},{3,11},{4,12},{5,13},{6,14},{7,15},{8,0},{9,1},... | collective-permute-start | bytes 663560 | tf_op jit(solution)/shard_map/ppermute | solution.py:462
  309.2 8.3 %collective-permute-start.16 = (bf16[2,9,48,128]{3,2,1,0:T(8,128)(2,1)S(1)}, bf16[2,9,48,128]{3,2,1,0:T(8,128)(2,1)S(1)}, u32[]{:S(2)}, u32[]{:S(2)}) collective-permute-start(bf16[2,9,48,128]{3,2,1,0:T(8,128)(2,1)S(1)} %slice_bitcast_fusion.13), channel_id=1, source_target_pairs={{0,16},{1,17},{2,18},{3,19},{4,20},{5,21},{6,22},{7,23},{8,24},{9,... | collective-permute-start | bytes 663560 | tf_op jit(solution)/shard_map/ppermute | solution.py:462
  313.9 9.1 %collective-permute-start.19 = (bf16[2,9,48,128]{3,2,1,0:T(8,128)(2,1)S(1)}, bf16[2,9,48,128]{3,2,1,0:T(8,128)(2,1)S(1)}, u32[]{:S(2)}, u32[]{:S(2)}) collective-permute-start(bf16[2,9,48,128]{3,2,1,0:T(8,128)(2,1)S(1)} %fusion.30), channel_id=1, source_target_pairs={{0,4},{1,5},{2,6},{3,7},{4,0},{5,1},{6,2},{7,3},{8,12},{9,13},{10,... | collective-permute-start | bytes 663560 | tf_op jit(solution)/shard_map/ppermute | solution.py:462
  316.8 6.4 %collective-permute-start.31 = (bf16[2,3,48,128]{3,2,1,0:T(8,128)(2,1)S(1)}, bf16[2,3,48,128]{3,2,1,0:T(8,128)(2,1)S(1)}, u32[]{:S(2)}, u32[]{:S(2)}) collective-permute-start(bf16[2,3,48,128]{3,2,1,0:T(8,128)(2,1)S(1)} %get-tuple-element.81), channel_id=1, source_target_pairs={{0,16},{1,17},{2,18},{3,19},{4,20},{5,21},{6,22},{7,23},{8,24},{9,... | collective-permute-start | bytes 221192 | tf_op jit(solution)/shard_map/ppermute | solution.py:462
  323.1 4.8 %collective-permute-start.20 = (bf16[9,48,128]{2,1,0:T(8,128)(2,1)S(1)}, bf16[9,48,128]{2,1,0:T(8,128)(2,1)S(1)}, u32[]{:S(2)}, u32[]{:S(2)}) collective-permute-start(bf16[9,48,128]{2,1,0:T(8,128)(2,1)S(1)} %slice_bitcast_fusion.20), channel_id=1, source_target_pairs={{0,2},{1,3},{2,0},{3,1},{4,6},{5,7},{6,4},{7,5},{8,10},{9,11},{10,... | collective-permute-start | bytes 331784 | tf_op jit(solution)/shard_map/ppermute | solution.py:462
  328.0 4.8 %collective-permute-start.21 = (bf16[9,48,128]{2,1,0:T(8,128)(2,1)S(1)}, bf16[9,48,128]{2,1,0:T(8,128)(2,1)S(1)}, u32[]{:S(2)}, u32[]{:S(2)}) collective-permute-start(bf16[9,48,128]{2,1,0:T(8,128)(2,1)S(1)} %fusion.38), channel_id=1, source_target_pairs={{0,8},{1,9},{2,10},{3,11},{4,12},{5,13},{6,14},{7,15},{8,0},{9,1},... | collective-permute-start | bytes 331784 | tf_op jit(solution)/shard_map/ppermute | solution.py:462
  332.8 8.4 %collective-permute-start.22 = (bf16[2,9,48,128]{3,2,1,0:T(8,128)(2,1)S(1)}, bf16[2,9,48,128]{3,2,1,0:T(8,128)(2,1)S(1)}, u32[]{:S(2)}, u32[]{:S(2)}) collective-permute-start(bf16[2,9,48,128]{3,2,1,0:T(8,128)(2,1)S(1)} %get-tuple-element.79), channel_id=1, source_target_pairs={{0,16},{1,17},{2,18},{3,19},{4,20},{5,21},{6,22},{7,23},{8,24},{9,... | collective-permute-start | bytes 663560 | tf_op jit(solution)/shard_map/ppermute | solution.py:462
  342.6 15.9 %collective-permute-start.44 = (bf16[2,2,3,3,64,128]{5,4,3,2,1,0:T(8,128)(2,1)S(1)}, bf16[2,2,3,3,64,128]{5,4,3,2,1,0:T(8,128)(2,1)S(1)}, u32[]{:S(2)}, u32[]{:S(2)}) collective-permute-start(bf16[2,2,3,3,64,128]{5,4,3,2,1,0:T(8,128)(2,1)S(1)} %fusion.21), channel_id=1, source_target_pairs={{0,16},{1,17},{2,18},{3,19},{4,20},{5,21},{6,22},{7,23},{8,24},{9,... | collective-permute-start | bytes 1769480 | tf_op jit(solution)/shard_map/ppermute | solution.py:462
  344.1 14.7 %collective-permute-start.42 = (bf16[2,2,3,3,64,128]{5,4,3,2,1,0:T(8,128)(2,1)S(1)}, bf16[2,2,3,3,64,128]{5,4,3,2,1,0:T(8,128)(2,1)S(1)}, u32[]{:S(2)}, u32[]{:S(2)}) collective-permute-start(bf16[2,2,3,3,64,128]{5,4,3,2,1,0:T(8,128)(2,1)S(1)} %fusion.18), channel_id=1, source_target_pairs={{0,8},{1,9},{2,10},{3,11},{4,12},{5,13},{6,14},{7,15},{8,0},{9,1},... | collective-permute-start | bytes 1769480 | tf_op jit(solution)/shard_map/ppermute | solution.py:462
  347.0 20.0 %collective-permute-start.35 = (bf16[2,2,12,48,128]{4,3,2,1,0:T(8,128)(2,1)S(1)}, bf16[2,2,12,48,128]{4,3,2,1,0:T(8,128)(2,1)S(1)}, u32[]{:S(2)}, u32[]{:S(2)}) collective-permute-start(bf16[2,2,12,48,128]{4,3,2,1,0:T(8,128)(2,1)S(1)} %fusion.20), channel_id=1, source_target_pairs={{0,16},{1,17},{2,18},{3,19},{4,20},{5,21},{6,22},{7,23},{8,24},{9,... | collective-permute-start | bytes 1769480 | tf_op jit(solution)/shard_map/ppermute | solution.py:462
  350.1 17.0 %collective-permute-start.33 = (bf16[2,2,12,48,128]{4,3,2,1,0:T(8,128)(2,1)S(1)}, bf16[2,2,12,48,128]{4,3,2,1,0:T(8,128)(2,1)S(1)}, u32[]{:S(2)}, u32[]{:S(2)}) collective-permute-start(bf16[2,2,12,48,128]{4,3,2,1,0:T(8,128)(2,1)S(1)} %fusion.15), channel_id=1, source_target_pairs={{0,8},{1,9},{2,10},{3,11},{4,12},{5,13},{6,14},{7,15},{8,0},{9,1},... | collective-permute-start | bytes 1769480 | tf_op jit(solution)/shard_map/ppermute | solution.py:462
  360.9 9.3 %collective-permute-start.45 = (bf16[2,3,3,64,128]{4,3,2,1,0:T(8,128)(2,1)S(1)}, bf16[2,3,3,64,128]{4,3,2,1,0:T(8,128)(2,1)S(1)}, u32[]{:S(2)}, u32[]{:S(2)}) collective-permute-start(bf16[2,3,3,64,128]{4,3,2,1,0:T(8,128)(2,1)S(1)} %slice_bitcast_fusion.3), channel_id=1, source_target_pairs={{0,8},{1,9},{2,10},{3,11},{4,12},{5,13},{6,14},{7,15},{8,0},{9,1},... | collective-permute-start | bytes 884744 | tf_op jit(solution)/shard_map/ppermute | solution.py:462
  362.2 15.3 %collective-permute-start.43 = (bf16[2,3,3,64,128]{4,3,2,1,0:T(8,128)(2,1)S(1)}, bf16[2,3,3,64,128]{4,3,2,1,0:T(8,128)(2,1)S(1)}, u32[]{:S(2)}, u32[]{:S(2)}) collective-permute-start(bf16[2,3,3,64,128]{4,3,2,1,0:T(8,128)(2,1)S(1)} %slice_bitcast_fusion.5), channel_id=1, source_target_pairs={{0,16},{1,17},{2,18},{3,19},{4,20},{5,21},{6,22},{7,23},{8,24},{9,... | collective-permute-start | bytes 884744 | tf_op jit(solution)/shard_map/ppermute | solution.py:462
  368.9 8.4 %collective-permute-start.36 = (bf16[2,12,48,128]{3,2,1,0:T(8,128)(2,1)S(1)}, bf16[2,12,48,128]{3,2,1,0:T(8,128)(2,1)S(1)}, u32[]{:S(2)}, u32[]{:S(2)}) collective-permute-start(bf16[2,12,48,128]{3,2,1,0:T(8,128)(2,1)S(1)} %slice_bitcast_fusion.7), channel_id=1, source_target_pairs={{0,8},{1,9},{2,10},{3,11},{4,12},{5,13},{6,14},{7,15},{8,0},{9,1},... | collective-permute-start | bytes 884744 | tf_op jit(solution)/shard_map/ppermute | solution.py:462
  370.3 10.6 %collective-permute-start.46 = (bf16[2,3,3,64,128]{4,3,2,1,0:T(8,128)(2,1)S(1)}, bf16[2,3,3,64,128]{4,3,2,1,0:T(8,128)(2,1)S(1)}, u32[]{:S(2)}, u32[]{:S(2)}) collective-permute-start(bf16[2,3,3,64,128]{4,3,2,1,0:T(8,128)(2,1)S(1)} %fusion.22), channel_id=1, source_target_pairs={{0,4},{1,5},{2,6},{3,7},{4,0},{5,1},{6,2},{7,3},{8,12},{9,13},{10,... | collective-permute-start | bytes 884744 | tf_op jit(solution)/shard_map/ppermute | solution.py:462
  370.8 12.9 %collective-permute-start.34 = (bf16[2,12,48,128]{3,2,1,0:T(8,128)(2,1)S(1)}, bf16[2,12,48,128]{3,2,1,0:T(8,128)(2,1)S(1)}, u32[]{:S(2)}, u32[]{:S(2)}) collective-permute-start(bf16[2,12,48,128]{3,2,1,0:T(8,128)(2,1)S(1)} %slice_bitcast_fusion.9), channel_id=1, source_target_pairs={{0,16},{1,17},{2,18},{3,19},{4,20},{5,21},{6,22},{7,23},{8,24},{9,... | collective-permute-start | bytes 884744 | tf_op jit(solution)/shard_map/ppermute | solution.py:462
  377.4 10.3 %collective-permute-start.37 = (bf16[2,12,48,128]{3,2,1,0:T(8,128)(2,1)S(1)}, bf16[2,12,48,128]{3,2,1,0:T(8,128)(2,1)S(1)}, u32[]{:S(2)}, u32[]{:S(2)}) collective-permute-start(bf16[2,12,48,128]{3,2,1,0:T(8,128)(2,1)S(1)} %fusion.24), channel_id=1, source_target_pairs={{0,4},{1,5},{2,6},{3,7},{4,0},{5,1},{6,2},{7,3},{8,12},{9,13},{10,... | collective-permute-start | bytes 884744 | tf_op jit(solution)/shard_map/ppermute | solution.py:462
  381.1 8.0 %collective-permute-start.47 = (bf16[3,3,64,128]{3,2,1,0:T(8,128)(2,1)S(1)}, bf16[3,3,64,128]{3,2,1,0:T(8,128)(2,1)S(1)}, u32[]{:S(2)}, u32[]{:S(2)}) collective-permute-start(bf16[3,3,64,128]{3,2,1,0:T(8,128)(2,1)S(1)} %slice_bitcast_fusion.15), channel_id=1, source_target_pairs={{0,2},{1,3},{2,0},{3,1},{4,6},{5,7},{6,4},{7,5},{8,10},{9,11},{10,... | collective-permute-start | bytes 442376 | tf_op jit(solution)/shard_map/ppermute | solution.py:462
  387.8 5.2 %collective-permute-start.38 = (bf16[12,48,128]{2,1,0:T(8,128)(2,1)S(1)}, bf16[12,48,128]{2,1,0:T(8,128)(2,1)S(1)}, u32[]{:S(2)}, u32[]{:S(2)}) collective-permute-start(bf16[12,48,128]{2,1,0:T(8,128)(2,1)S(1)} %slice_bitcast_fusion.17), channel_id=1, source_target_pairs={{0,2},{1,3},{2,0},{3,1},{4,6},{5,7},{6,4},{7,5},{8,10},{9,11},{10,... | collective-permute-start | bytes 442376 | tf_op jit(solution)/shard_map/ppermute | solution.py:462
  389.2 5.2 %collective-permute-start.48 = (bf16[3,3,64,128]{3,2,1,0:T(8,128)(2,1)S(1)}, bf16[3,3,64,128]{3,2,1,0:T(8,128)(2,1)S(1)}, u32[]{:S(2)}, u32[]{:S(2)}) collective-permute-start(bf16[3,3,64,128]{3,2,1,0:T(8,128)(2,1)S(1)} %fusion.32), channel_id=1, source_target_pairs={{0,8},{1,9},{2,10},{3,11},{4,12},{5,13},{6,14},{7,15},{8,0},{9,1},... | collective-permute-start | bytes 442376 | tf_op jit(solution)/shard_map/ppermute | solution.py:462
  393.0 5.2 %collective-permute-start.39 = (bf16[12,48,128]{2,1,0:T(8,128)(2,1)S(1)}, bf16[12,48,128]{2,1,0:T(8,128)(2,1)S(1)}, u32[]{:S(2)}, u32[]{:S(2)}) collective-permute-start(bf16[12,48,128]{2,1,0:T(8,128)(2,1)S(1)} %fusion.33), channel_id=1, source_target_pairs={{0,8},{1,9},{2,10},{3,11},{4,12},{5,13},{6,14},{7,15},{8,0},{9,1},... | collective-permute-start | bytes 442376 | tf_op jit(solution)/shard_map/ppermute | solution.py:462
  394.4 6.8 %collective-permute-start.49 = (bf16[2,3,3,64,128]{4,3,2,1,0:T(8,128)(2,1)S(1)}, bf16[2,3,3,64,128]{4,3,2,1,0:T(8,128)(2,1)S(1)}, u32[]{:S(2)}, u32[]{:S(2)}) collective-permute-start(bf16[2,3,3,64,128]{4,3,2,1,0:T(8,128)(2,1)S(1)} %get-tuple-element.75), channel_id=1, source_target_pairs={{0,16},{1,17},{2,18},{3,19},{4,20},{5,21},{6,22},{7,23},{8,24},{9,... | collective-permute-start | bytes 884744 | tf_op jit(solution)/shard_map/ppermute | solution.py:462
  398.3 6.8 %collective-permute-start.40 = (bf16[2,12,48,128]{3,2,1,0:T(8,128)(2,1)S(1)}, bf16[2,12,48,128]{3,2,1,0:T(8,128)(2,1)S(1)}, u32[]{:S(2)}, u32[]{:S(2)}) collective-permute-start(bf16[2,12,48,128]{3,2,1,0:T(8,128)(2,1)S(1)} %get-tuple-element.77), channel_id=1, source_target_pairs={{0,16},{1,17},{2,18},{3,19},{4,20},{5,21},{6,22},{7,23},{8,24},{9,... | collective-permute-start | bytes 884744 | tf_op jit(solution)/shard_map/ppermute | solution.py:462
  (30 other events, 279.1 us)
Sparse Core Ops, SparseCore 0:
  9.7 44.2 all-gather.4
  55.6 21.9 all-gather.6
  79.2 50.8 all-gather.10
  131.6 49.9 all-gather.8
